TPU v7x, 256 devices: a whole 4x4x8 slice. The times are simulated.
256 devices in a mesh: chan: 32 (over z, y_hi, core), tm: 8 (over y_lo, x).
Axes of the slice: x: 4, y: 4 (y_hi: 2, y_lo: 2; y = y_hi * 2 + y_lo), z: 8, core: 2. Of those that a mesh axis runs over, the one named last changes fastest.
Arguments:
- traces: bfloat16 [32, 192, 128, 1024], P('chan', 'tm'), may hold values from -6 to 6
- valid_mask: int32 [32, 192, 1024], P('chan', 'tm'), may hold values 0 or 1
- pair_owner: int32 [32, 4], P('chan'), may hold values from -1 to 31, as said below
Outputs:
- correlations: float32 [32, 4, 101, 128], P('chan')
Inputs may be any that keep to these rules, and one draw needn't show every extreme that they name: `pair_owner`: row r lists distinct owners in r + 1 .. r + 4 (within the cable) in its leading slots, then -1; every reader with a block above it has one pair or more, and reader 0 fills all 4 slots.
All inputs are finite; a program needn't handle non-finite values. No bound on the sum of `valid_mask` on one device may be relied on, other than what follows from the above.
Results may differ from a plain program's by a relative error of at most 0.0052.
Values may be sent and summed in bfloat16 or wider, within the bound.
No kernel may reach another device: no remote copies, remote signals or barrier semaphores. Data moves between devices by JAX's collectives and lax.ppermute only.
A program may use at most 64 MiB of HBM per device.

v0:
```python
import functools
import math

import jax
import jax.numpy as jnp
import numpy as np
from jax import lax
from jax.experimental import pallas as pl
from jax.experimental.pallas import tpu as pltpu
from jax.sharding import PartitionSpec as P

NF = 256
WIN = 1024
MAXLAG = 50
SMOOTH = 4
REACH = 4
LAGS = 2 * MAXLAG + 1
ROWS = 104
TABLE_ROWS = 112
HALF = 64
STEP = 3
TILE = 16
PLANES = 12
CHUNKS = ((0, 6), (6, 9), (15, 6), (21, 3))
GROUPS = ((0, 1), (2,), (3,))
VMEM = 24 << 20
WATER = 0.05
EPS = 1e-06


f32 = jnp.float32
bf16 = jnp.bfloat16


def forward_table():
    samples = np.arange(WIN, dtype=np.int32)
    bins = np.arange(1, NF + 1, dtype=np.int32)
    phase = samples[:, None] * bins[None, :] % WIN
    angle = phase.astype(np.float32) * np.float32(2.0 * math.pi / WIN)
    return np.concatenate([np.cos(angle), -np.sin(angle)], axis=1).astype(bf16)


def inverse_tables(windows_all):
    bins = np.arange(1, NF + 1, dtype=np.int32)
    offsets = np.arange(LAGS, dtype=np.int32) - MAXLAG
    phase = bins[None, :] * offsets[:, None] % WIN
    angle = phase.astype(np.float32) * np.float32(2.0 * math.pi / WIN)
    factor = np.float32(1.0 / math.sqrt(windows_all * NF))
    table = np.concatenate([np.cos(angle), -np.sin(angle)], axis=1) * factor
    table = np.pad(table, ((0, TABLE_ROWS - LAGS), (0, 0))).astype(np.float32)
    high = table.astype(bf16)
    low = (table - high.astype(np.float32)).astype(bf16)
    return high, low


def band_table():
    bins = np.arange(NF)
    near = np.abs(bins[:, None] - bins[None, :]) <= SMOOTH
    return np.concatenate([near, near], axis=0).astype(bf16)


def prepare(role, traces, mask, first, count):
    step = STEP
    base = first // step

    def kernel(role, traces, mask, out):
        i = pl.program_id(0)
        for j in range(step):
            keep = mask[pl.ds(first + i * step + j, 1), :].astype(f32).astype(bf16)
            out[j] = traces[j] * keep

    return pl.pallas_call(
        kernel,
        grid_spec=pltpu.PrefetchScalarGridSpec(
            num_scalar_prefetch=1,
            grid=(count // step,),
            in_specs=[
                pl.BlockSpec((step, HALF, WIN), lambda i, role: (base + i, 1 - role[1], 0)),
                pl.BlockSpec(mask.shape, lambda i, role: (0, 0)),
            ],
            out_specs=pl.BlockSpec((step, HALF, WIN), lambda i, role: (i, 0, 0)),
        ),
        out_shape=jax.ShapeDtypeStruct((count, HALF, WIN), bf16),
        compiler_params=pltpu.CompilerParams(vmem_limit_bytes=VMEM),
        cost_estimate=pl.CostEstimate(
            flops=count * HALF * WIN, bytes_accessed=4 * count * HALF * WIN, transcendentals=0
        ),
    )(role, traces, mask)


def whiten_kernel(first, role, traces, given, mask, forward, band, out, masked, spectra, split, level):
    step = pl.program_id(0)
    core = role[1]
    for j in range(STEP):
        keep = mask[pl.ds(first + step * STEP + j, 1), :].astype(f32).astype(bf16)
        masked[j * HALF : (j + 1) * HALF, :] = traces[j] * keep
        masked[(STEP + j) * HALF : (STEP + j + 1) * HALF, :] = given[j]
    spectra[...] = jnp.dot(masked[...], forward[...], preferred_element_type=f32)
    for r in range(0, 2 * STEP * HALF, 32):
        rows = slice(r, r + 32)
        real = spectra[rows, :NF]
        imag = spectra[rows, NF:]
        amplitude = jnp.sqrt(real * real + imag * imag)
        high = amplitude.astype(bf16)
        split[rows, :NF] = high
        split[rows, NF:] = (amplitude - high.astype(f32)).astype(bf16)
        total = jnp.sum(amplitude, axis=-1, keepdims=True)
        level[rows, :] = jnp.broadcast_to(total * f32(WATER / NF) + f32(EPS), (32, 128))
    smooth = jnp.dot(split[...], band[...], preferred_element_type=f32)
    for r in range(0, 2 * STEP * HALF, 32):
        rows = slice(r, r + 32)
        base = level[rows, :]
        divisor = smooth[rows, :] * f32(1.0 / (2 * SMOOTH + 1)) + jnp.concatenate([base, base], axis=1)
        inverse = 1.0 / divisor
        h, rest = divmod(r, STEP * HALF)
        j, c = divmod(rest, HALF)
        block = core if h == 0 else 1 - core
        out[block, j, c : c + 32, :NF] = (spectra[rows, :NF] * inverse).astype(bf16)
        out[block, j, c : c + 32, NF:] = (spectra[rows, NF:] * inverse).astype(bf16)


def whiten(role, traces, given, mask, forward, band, first, count, skip):
    rows = 2 * STEP * HALF
    base = first // STEP
    skip = skip // STEP
    return pl.pallas_call(
        functools.partial(whiten_kernel, first),
        grid_spec=pltpu.PrefetchScalarGridSpec(
            num_scalar_prefetch=1,
            grid=(count // STEP,),
            in_specs=[
                pl.BlockSpec((STEP, HALF, WIN), lambda i, role: (base + i, role[1], 0)),
                pl.BlockSpec((STEP, HALF, WIN), lambda i, role: (skip + i, 0, 0)),
                pl.BlockSpec(mask.shape, lambda i, role: (0, 0)),
                pl.BlockSpec(forward.shape, lambda i, role: (0, 0)),
                pl.BlockSpec(band.shape, lambda i, role: (0, 0)),
            ],
            out_specs=pl.BlockSpec((2, STEP, HALF, 2 * NF), lambda i, role: (0, i, 0, 0)),
            scratch_shapes=[
                pltpu.VMEM((rows, WIN), bf16),
                pltpu.VMEM((rows, 2 * NF), f32),
                pltpu.VMEM((rows, 2 * NF), bf16),
                pltpu.VMEM((rows, 128), f32),
            ],
        ),
        out_shape=jax.ShapeDtypeStruct((2, count, HALF, 2 * NF), bf16),
        compiler_params=pltpu.CompilerParams(vmem_limit_bytes=VMEM),
        cost_estimate=pl.CostEstimate(
            flops=2 * count * 2 * HALF * (WIN * 2 * NF + 2 * NF * NF),
            bytes_accessed=count * 2 * HALF * (WIN + 2 * NF) * 2,
            transcendentals=count * 2 * HALF * NF * 2,
        ),
    )(role, traces, given, mask, forward, band)


def cross_kernel(counts, start, last, role, *refs):
    sets = [refs[3 * k : 3 * k + 3] for k in range(len(counts))]
    refs = refs[3 * len(counts) :]
    before = None
    if not start:
        before, refs = refs[0], refs[1:]
    table_high, table_low, *refs = refs
    if last:
        kept, to_z, to_y, buf, sem, total = refs
    else:
        kept, buf, sem, total = refs
    y_hi = role[0]
    core = role[1]
    tiles = HALF // TILE
    offsets = [sum(counts[:k]) for k in range(len(counts))]

    def copy(source, k, t, slot):
        place = buf.at[t, pl.ds(slot, 2), pl.ds(offsets[k], counts[k])]
        return pltpu.make_async_copy(source.at[:, :, pl.ds(t * TILE, TILE), :], place, sem.at[k, t, slot // 2])

    for t in range(tiles):
        for k, (own, near, across) in enumerate(sets):
            copy(across, k, t, 4).start()

            @pl.when(core == 0)
            def _():
                copy(own, k, t, 0).start()
                copy(near, k, t, 2).start()

            @pl.when(core != 0)
            def _():
                copy(near, k, t, 0).start()
                copy(own, k, t, 2).start()

    count = sum(counts)
    zero = jnp.zeros((TILE, 128), f32)

    def tile(t, carry):
        for k in range(len(counts)):
            for slot in (0, 2, 4):
                copy(sets[k][2], k, t, slot).wait()
        rows = pl.ds(pl.multiple_of(t * TILE, TILE), TILE)
        for f in range(0, NF, 128):
            re = slice(f, f + 128)
            im = slice(NF + f, NF + f + 128)

            def run(pairs):
                slots = sorted({s for _, a, b in pairs for s in (a, b)})

                def window(w, sums):
                    at = {s: (buf[t, s, w, :, re].astype(f32), buf[t, s, w, :, im].astype(f32)) for s in slots}
                    out = []
                    for (_, a, b), (sr, si) in zip(pairs, sums):
                        ar, ai = at[a]
                        br, bi = at[b]
                        out.append((sr + (ar * br + ai * bi), si + (ar * bi - ai * br)))
                    return tuple(out)

                sums = lax.fori_loop(0, count, window, tuple((zero, zero) for _ in pairs), unroll=3)
                for (plane, _, _), (sr, si) in zip(pairs, sums):
                    total[plane, rows, re] = sr
                    total[plane, rows, im] = si

            inner = ((3, 0, 2), (6, 1, 2), (7, 1, 3))

            @pl.when(core == 0)
            def _():
                run(((0, 0, 1), *inner))

            @pl.when(core != 0)
            def _():
                run(((0, 2, 3), *inner))

            @pl.when(y_hi == core)
            def _():
                run(((1, 0, 4), (2, 0, 5), (4, 1, 4), (5, 1, 5)))
                run(((8, 4, 2), (9, 4, 3), (10, 5, 2), (11, 5, 3)))

            @pl.when(y_hi != core)
            def _():
                for plane in (1, 2, 4, 5, 8, 9, 10, 11):
                    total[plane, rows, re] = zero
                    total[plane, rows, im] = zero

        return carry

    lax.fori_loop(0, tiles, tile, 0)
    stack = total[...].reshape(PLANES * HALF, 2 * NF)
    high = stack.astype(bf16)
    low = (stack - high.astype(f32)).astype(bf16)
    dims = (((1,), (1,)), ((), ()))
    dot = functools.partial(lax.dot_general, dimension_numbers=dims, preferred_element_type=f32)
    result = dot(table_high[...], high) + dot(table_high[...], low) + dot(table_low[...], high)
    result = result[:ROWS]
    if not start:
        result = result + before[...]
    if not last:
        kept[...] = result
        return
    near_part = result[:, : 8 * HALF]
    lane = lax.broadcasted_iota(jnp.int32, near_part.shape, 1)
    local = lane < HALF
    kept[...] = jnp.where((lane < jnp.where(core == 0, 8 * HALF, HALF)), near_part, 0.0)
    to_z[...] = jnp.where(local, 0.0, near_part).astype(bf16)
    to_y[...] = result[:, 8 * HALF :].astype(bf16)


def whole(shape):
    return pl.BlockSpec(shape, lambda i, role: (0,) * len(shape))


def cross(role, sets, before, tables, last):
    counts = tuple(s[0].shape[1] for s in sets)
    start = before is None
    args = [a for s in sets for a in s]
    in_specs = [pl.BlockSpec(memory_space=pl.ANY)] * len(args)
    if not start:
        args.append(before)
        in_specs.append(whole(before.shape))
    args += list(tables)
    in_specs += [whole((TABLE_ROWS, 2 * NF))] * 2
    tiles = HALF // TILE
    scratch = [
        pltpu.VMEM((tiles, 6, sum(counts), TILE, 2 * NF), bf16),
        pltpu.SemaphoreType.DMA((len(counts), tiles, 3)),
        pltpu.VMEM((PLANES, HALF, 2 * NF), f32),
    ]
    if last:
        out_shape = [
            jax.ShapeDtypeStruct((ROWS, 8 * HALF), f32),
            jax.ShapeDtypeStruct((ROWS, 8 * HALF), bf16),
            jax.ShapeDtypeStruct((ROWS, 4 * HALF), bf16),
        ]
        out_specs = [whole(s.shape) for s in out_shape]
    else:
        out_shape = jax.ShapeDtypeStruct((ROWS, PLANES * HALF), f32)
        out_specs = whole(out_shape.shape)
    return pl.pallas_call(
        functools.partial(cross_kernel, counts, start, last),
        grid_spec=pltpu.PrefetchScalarGridSpec(
            num_scalar_prefetch=1, grid=(1,), in_specs=in_specs, out_specs=out_specs, scratch_shapes=scratch
        ),
        out_shape=out_shape,
        compiler_params=pltpu.CompilerParams(vmem_limit_bytes=VMEM),
        cost_estimate=pl.CostEstimate(
            flops=PLANES * 8 * sum(counts) * HALF * NF,
            bytes_accessed=6 * sum(counts) * HALF * 2 * NF * 2,
            transcendentals=0,
        ),
        name="cross_last" if last else "cross_first" if start else "cross_middle",
    )(role, *args)


def combine_kernel(role, kept, from_z, from_y, own, give):
    core = role[1]
    y = from_y[...].astype(f32)
    gap = jnp.zeros((ROWS, HALF), f32)
    placed = jnp.concatenate([gap, y[:, : 2 * HALF], gap, y[:, 2 * HALF :], gap, gap], axis=1)
    total = (kept[...] + from_z[...].astype(f32) + placed).astype(bf16)
    first, second = total[:, : 4 * HALF].astype(f32), total[:, 4 * HALF :].astype(f32)
    own[...] = jnp.where(core == 0, first, second).astype(bf16)
    give[...] = jnp.where(core == 0, second, first).astype(bf16)


def combine(role, kept, from_z, from_y):
    part = jax.ShapeDtypeStruct((ROWS, 4 * HALF), bf16)
    return pl.pallas_call(
        combine_kernel,
        grid_spec=pltpu.PrefetchScalarGridSpec(
            num_scalar_prefetch=1,
            grid=(1,),
            in_specs=[whole(a.shape) for a in (kept, from_z, from_y)],
            out_specs=[whole(part.shape)] * 2,
        ),
        out_shape=[part, part],
        compiler_params=pltpu.CompilerParams(vmem_limit_bytes=VMEM),
        name="combine",
    )(role, kept, from_z, from_y)


def assemble_kernel(role, slots, own, got, out):
    core = role[1]
    mine, other = own[...].astype(f32), got[...].astype(f32)
    first = jnp.where(core == 0, mine, other)
    second = jnp.where(core == 0, other, mine)
    planes = [
        jnp.concatenate([first[:, i * HALF : (i + 1) * HALF], second[:, i * HALF : (i + 1) * HALF]], axis=1)
        for i in range(REACH)
    ]
    for slot in range(REACH):
        distance = slots[slot]
        value = jnp.zeros((ROWS, 2 * HALF), f32)
        for k in range(REACH):
            value = jnp.where(distance == k + 1, planes[k], value)
        out[:, slot * 2 * HALF : (slot + 1) * 2 * HALF] = value.astype(bf16)


def assemble(role, slots, own, got):
    shape = (ROWS, REACH * 2 * HALF)
    return pl.pallas_call(
        assemble_kernel,
        grid_spec=pltpu.PrefetchScalarGridSpec(
            num_scalar_prefetch=2,
            grid=(1,),
            in_specs=[pl.BlockSpec(own.shape, lambda i, *_: (0, 0)), pl.BlockSpec(got.shape, lambda i, *_: (0, 0))],
            out_specs=pl.BlockSpec(shape, lambda i, *_: (0, 0)),
        ),
        out_shape=jax.ShapeDtypeStruct(shape, bf16),
        compiler_params=pltpu.CompilerParams(vmem_limit_bytes=VMEM),
        name="assemble",
    )(role, slots, own, got)


def route(blocks, times, target):
    pairs = []
    for b in range(blocks):
        z, y_hi, core = b // 4, b // 2 % 2, b % 2
        for t in range(times):
            to_z, to_y, to_core, to_t = target(z, y_hi, core, t)
            if 0 <= to_z < blocks // 4:
                pairs.append((b * times + t, ((to_z * 2 + to_y) * 2 + to_core) * times + to_t))
    return pairs


def body(traces, valid_mask, pair_owner):
    blocks, times = lax.axis_size("chan"), lax.axis_size("tm")
    windows_all = traces.shape[1] * times

    def move(block, target):
        return lax.ppermute(block, ("chan", "tm"), route(blocks, times, target))

    def to_core(block):
        return move(block, lambda z, y, c, t: (z, y, 1 - c, t))

    reader = lax.axis_index("chan")
    core = reader % 2
    role = jnp.where(jnp.arange(2, dtype=jnp.int32) == 0, reader // 2 % 2, core)
    slots = pair_owner[0] - reader
    forward, band = jnp.asarray(forward_table()), jnp.asarray(band_table())
    high, low = inverse_tables(windows_all)
    tables = (jnp.asarray(high), jnp.asarray(low))
    mask = valid_mask[0]

    rest = CHUNKS[0][1]
    later = traces.shape[1] - rest
    head = prepare(role, traces[0], mask, 0, rest)
    head = to_core(head)
    body_part = prepare(role, traces[0], mask, rest, later)
    body_part = to_core(body_part)
    sets = []
    order = role
    for k, (first, count) in enumerate(CHUNKS):
        given, skip = (head, 0) if k == 0 else (body_part, first - rest)
        own = whiten(order, traces[0], given, mask, forward, band, first, count, skip)
        own, order = lax.optimization_barrier((own, order))
        near = move(own, lambda z, y, c, t: (z - 1 + 2 * c, y, c, t))
        across = move(own, lambda z, y, c, t: (z, 1 - y, c, t) if y != c else (-1, y, c, t))
        sets.append((own, near, across))
    stack = None
    for k, group in enumerate(GROUPS):
        stack = cross(order, [sets[i] for i in group], stack, tables, k == len(GROUPS) - 1)
    kept, for_z, for_y = stack
    from_z = move(for_z, lambda z, y, c, t: (z - 1 if c else -1, y, c, t))
    from_y = move(for_y, lambda z, y, c, t: (z if y == c else -1, 1 - y, c, t))
    mine, give = combine(role, kept, from_z, from_y)
    partial = assemble(role, slots, mine, to_core(give))
    for bit in (4, 1, 2):
        arrived = move(partial, lambda z, y, c, t: (z, y, c, t ^ bit))
        partial = partial.astype(f32) + arrived.astype(f32)
        if bit != 2:
            partial = partial.astype(bf16)
    result = partial[:LAGS].reshape(LAGS, REACH, 2 * HALF)
    return result.transpose(1, 0, 2)[None]


def solution(mesh):
    return jax.shard_map(
        body,
        mesh=mesh,
        in_specs=(P("chan", "tm", None, None), P("chan", "tm", None), P("chan", None)),
        out_specs=P("chan", None, None, None),
        check_vma=False,
    )
```

profile of v0, /device:TPU:32, one launch (start us, length us, event | category | flops | bytes accessed | tf_op | source)
XLA Modules:
  0.0 97.9 jit_solution(3834731705585392854)
XLA Ops:
  0.0 2.8 %copy-done = bf16[1,24,128,1024]{3,2,1,0:T(8,128)(2,1)S(1)} copy-done((bf16[1,24,128,1024]{3,2,1,0:T(8,128)(2,1)S(1)}, bf16[1,24,128,1024]{3,2,1,0:T(8,128)(2,1)}, u32[]{:S(2)}) %copy-start) | copy-done | bytes 6291480
  2.8 0.9 copy-done.3
  3.7 1.1 %shard_map.75 = bf16[18,64,1024]{2,1,0:T(8,128)(2,1)S(1)} custom-call(s32[2]{0:T(128)S(1)} %compare_select_fusion.role, bf16[24,128,1024]{2,1,0:T(8,128)(2,1)S(1)} %bitcast.7, s32[24,1024]{1,0:T(8,128)S(1)} %bitcast.13), custom_call_target="tpu_custom_call" | custom-call | flops 1179648 | bytes 4718592 | tf_op jit(solution)/shard_map/pallas_call | solution.py:72
  4.9 0.7 shard_map.73
  6.2 4.3 %collective-permute-done.given = bf16[6,64,1024]{2,1,0:T(8,128)(2,1)S(1)} collective-permute-done((bf16[6,64,1024]{2,1,0:T(8,128)(2,1)S(1)}, bf16[6,64,1024]{2,1,0:T(8,128)(2,1)S(1)}, u32[]{:S(2)}, u32[]{:S(2)}) %collective-permute-start) | collective-permute-done | bytes 786464 | tf_op jit(solution)/shard_map/ppermute | solution.py:385
  10.6 2.6 %shard_map.74.refs_0_ = bf16[2,6,64,512]{3,2,1,0:T(8,128)(2,1)S(1)} custom-call(s32[2]{0:T(128)S(1)} %compare_select_fusion.role, bf16[24,128,1024]{2,1,0:T(8,128)(2,1)S(1)} %bitcast.9, bf16[6,64,1024]{2,1,0:T(8,128)(2,1)S(1)} %collective-permute-done.given, s32[24,1024]{1,0:T(8,128)S(1)} %bitcast.15, bf16[1024,512]{1,0:T(8,128)(2,1)S(1)} %copy-done.1, ...), custom_call_target="tpu_custom_call" | custom-call | flops 1006632960 | bytes 2359296 | tf_op jit(solution)/shard_map/pallas_call | solution.py:126
  13.2 3.7 %collective-permute-start.6 = (bf16[2,6,64,512]{3,2,1,0:T(8,128)(2,1)S(1)}, bf16[2,6,64,512]{3,2,1,0:T(8,128)(2,1)S(1)}, u32[]{:S(2)}, u32[]{:S(2)}) collective-permute-start(bf16[2,6,64,512]{3,2,1,0:T(8,128)(2,1)S(1)} %shard_map.74.refs_0_), channel_id=1, source_target_pairs={{8,40},{9,41},{10,42},{11,43},{12,44},{13,45},{14,46},{15,47},{24,... | collective-permute-start | bytes 2359304 | tf_op jit(solution)/shard_map/ppermute | solution.py:385
  16.9 3.7 %shard_map.76.refs_3_ = bf16[2,9,64,512]{3,2,1,0:T(8,128)(2,1)S(1)} custom-call(s32[2]{0:T(128)S(1)} %compare_select_fusion.role, bf16[24,128,1024]{2,1,0:T(8,128)(2,1)S(1)} %bitcast.10, bf16[18,64,1024]{2,1,0:T(8,128)(2,1)S(1)} %collective-permute-done.1.given, s32[24,1024]{1,0:T(8,128)S(1)} %bitcast.16, bf16[1024,512]{1,0:T(8,128)(2,1)S(1)} %copy-done.1, ...), custom_call_target="tpu_custom_call" | custom-call | flops 1509949440 | bytes 3538944 | tf_op jit(solution)/shard_map/pallas_call | solution.py:126
  20.6 1.9 %collective-permute-start.8 = (bf16[2,9,64,512]{3,2,1,0:T(8,128)(2,1)S(1)}, bf16[2,9,64,512]{3,2,1,0:T(8,128)(2,1)S(1)}, u32[]{:S(2)}, u32[]{:S(2)}) collective-permute-start(bf16[2,9,64,512]{3,2,1,0:T(8,128)(2,1)S(1)} %shard_map.76.refs_3_), channel_id=1, source_target_pairs={{8,40},{9,41},{10,42},{11,43},{12,44},{13,45},{14,46},{15,47},{24,... | collective-permute-start | bytes 3538952 | tf_op jit(solution)/shard_map/ppermute | solution.py:385
  22.5 1.3 %collective-permute-start.9 = (bf16[2,9,64,512]{3,2,1,0:T(8,128)(2,1)S(1)}, bf16[2,9,64,512]{3,2,1,0:T(8,128)(2,1)S(1)}, u32[]{:S(2)}, u32[]{:S(2)}) collective-permute-start(bf16[2,9,64,512]{3,2,1,0:T(8,128)(2,1)S(1)} %shard_map.76.refs_3_), channel_id=1, source_target_pairs={{8,24},{9,25},{10,26},{11,27},{12,28},{13,29},{14,30},{15,31},{16,... | collective-permute-start | bytes 3538952 | tf_op jit(solution)/shard_map/ppermute | solution.py:385
  23.8 1.3 %collective-permute-start.7 = (bf16[2,6,64,512]{3,2,1,0:T(8,128)(2,1)S(1)}, bf16[2,6,64,512]{3,2,1,0:T(8,128)(2,1)S(1)}, u32[]{:S(2)}, u32[]{:S(2)}) collective-permute-start(bf16[2,6,64,512]{3,2,1,0:T(8,128)(2,1)S(1)} %shard_map.74.refs_0_), channel_id=1, source_target_pairs={{8,24},{9,25},{10,26},{11,27},{12,28},{13,29},{14,30},{15,31},{16,... | collective-permute-start | bytes 2359304 | tf_op jit(solution)/shard_map/ppermute | solution.py:385
  25.1 2.6 %shard_map.77.refs_0_ = bf16[2,6,64,512]{3,2,1,0:T(8,128)(2,1)S(1)} custom-call(s32[2]{0:T(128)S(1)} %compare_select_fusion.role, bf16[24,128,1024]{2,1,0:T(8,128)(2,1)S(1)} %bitcast.11, bf16[18,64,1024]{2,1,0:T(8,128)(2,1)S(1)} %collective-permute-done.1.given, s32[24,1024]{1,0:T(8,128)S(1)} %bitcast.17, bf16[1024,512]{1,0:T(8,128)(2,1)S(1)} %copy-done.1, ...), custom_call_target="tpu_custom_call" | custom-call | flops 1006632960 | bytes 2359296 | tf_op jit(solution)/shard_map/pallas_call | solution.py:126
  27.8 2.1 %collective-permute-start.4 = (bf16[2,6,64,512]{3,2,1,0:T(8,128)(2,1)S(1)}, bf16[2,6,64,512]{3,2,1,0:T(8,128)(2,1)S(1)}, u32[]{:S(2)}, u32[]{:S(2)}) collective-permute-start(bf16[2,6,64,512]{3,2,1,0:T(8,128)(2,1)S(1)} %shard_map.77.refs_0_), channel_id=1, source_target_pairs={{8,40},{9,41},{10,42},{11,43},{12,44},{13,45},{14,46},{15,47},{24,... | collective-permute-start | bytes 2359304 | tf_op jit(solution)/shard_map/ppermute | solution.py:385
  29.9 1.3 %collective-permute-start.5 = (bf16[2,6,64,512]{3,2,1,0:T(8,128)(2,1)S(1)}, bf16[2,6,64,512]{3,2,1,0:T(8,128)(2,1)S(1)}, u32[]{:S(2)}, u32[]{:S(2)}) collective-permute-start(bf16[2,6,64,512]{3,2,1,0:T(8,128)(2,1)S(1)} %shard_map.77.refs_0_), channel_id=1, source_target_pairs={{8,24},{9,25},{10,26},{11,27},{12,28},{13,29},{14,30},{15,31},{16,... | collective-permute-start | bytes 2359304 | tf_op jit(solution)/shard_map/ppermute | solution.py:385
  31.2 1.5 %shard_map.78.refs_0_ = bf16[2,3,64,512]{3,2,1,0:T(8,128)(2,1)S(1)} custom-call(s32[2]{0:T(128)S(1)} %compare_select_fusion.role, bf16[24,128,1024]{2,1,0:T(8,128)(2,1)S(1)} %bitcast.12, bf16[18,64,1024]{2,1,0:T(8,128)(2,1)S(1)} %collective-permute-done.1.given, s32[24,1024]{1,0:T(8,128)S(1)} %bitcast.18, bf16[1024,512]{1,0:T(8,128)(2,1)S(1)} %copy-done.1, ...), custom_call_target="tpu_custom_call" | custom-call | flops 503316480 | bytes 1179648 | tf_op jit(solution)/shard_map/pallas_call | solution.py:126
  32.7 17.9 %collective-permute-done.7.refs_2_ = bf16[2,6,64,512]{3,2,1,0:T(8,128)(2,1)S(1)} collective-permute-done((bf16[2,6,64,512]{3,2,1,0:T(8,128)(2,1)S(1)}, bf16[2,6,64,512]{3,2,1,0:T(8,128)(2,1)S(1)}, u32[]{:S(2)}, u32[]{:S(2)}) %collective-permute-start.7) | collective-permute-done | bytes 786464 | tf_op jit(solution)/shard_map/ppermute | solution.py:385
  50.6 1.9 %collective-permute-start.2 = (bf16[2,3,64,512]{3,2,1,0:T(8,128)(2,1)S(1)}, bf16[2,3,64,512]{3,2,1,0:T(8,128)(2,1)S(1)}, u32[]{:S(2)}, u32[]{:S(2)}) collective-permute-start(bf16[2,3,64,512]{3,2,1,0:T(8,128)(2,1)S(1)} %shard_map.78.refs_0_), channel_id=1, source_target_pairs={{8,40},{9,41},{10,42},{11,43},{12,44},{13,45},{14,46},{15,47},{24,... | collective-permute-start | bytes 1179656 | tf_op jit(solution)/shard_map/ppermute | solution.py:385
  52.5 1.3 %collective-permute-start.3 = (bf16[2,3,64,512]{3,2,1,0:T(8,128)(2,1)S(1)}, bf16[2,3,64,512]{3,2,1,0:T(8,128)(2,1)S(1)}, u32[]{:S(2)}, u32[]{:S(2)}) collective-permute-start(bf16[2,3,64,512]{3,2,1,0:T(8,128)(2,1)S(1)} %shard_map.78.refs_0_), channel_id=1, source_target_pairs={{8,24},{9,25},{10,26},{11,27},{12,28},{13,29},{14,30},{15,31},{16,... | collective-permute-start | bytes 1179656 | tf_op jit(solution)/shard_map/ppermute | solution.py:385
  53.8 7.0 %cross_first.1.refs_3_ = f32[104,768]{1,0:T(8,128)S(1)} custom-call(s32[2]{0:T(128)S(1)} %compare_select_fusion.role, bf16[2,6,64,512]{3,2,1,0:T(8,128)(2,1)S(1)} %shard_map.74.refs_0_, bf16[2,6,64,512]{3,2,1,0:T(8,128)(2,1)S(1)} %collective-permute-done.6.refs_1_, bf16[2,6,64,512]{3,2,1,0:T(8,128)(2,1)S(1)} %collective-permute-done.7.refs_2_, ...), custom_call_target="tpu_custom_call" | custom-call | flops 23592960 | bytes 5898240 | tf_op jit(solution)/shard_map/cross_first/pallas_call | solution.py:293
  60.8 3.9 %cross_middle.1.refs_3_ = f32[104,768]{1,0:T(8,128)S(1)} custom-call(s32[2]{0:T(128)S(1)} %compare_select_fusion.role, bf16[2,6,64,512]{3,2,1,0:T(8,128)(2,1)S(1)} %shard_map.77.refs_0_, bf16[2,6,64,512]{3,2,1,0:T(8,128)(2,1)S(1)} %collective-permute-done.4.refs_1_, bf16[2,6,64,512]{3,2,1,0:T(8,128)(2,1)S(1)} %collective-permute-done.5.refs_2_, ...), custom_call_target="tpu_custom_call" | custom-call | flops 9437184 | bytes 2359296 | tf_op jit(solution)/shard_map/cross_middle/pallas_call | solution.py:293
  64.7 2.7 %cross_last.1 = (f32[104,512]{1,0:T(8,128)S(1)}, bf16[104,512]{1,0:T(8,128)(2,1)S(1)}, bf16[104,256]{1,0:T(8,128)(2,1)S(1)}) custom-call(s32[2]{0:T(128)S(1)} %compare_select_fusion.role, bf16[2,3,64,512]{3,2,1,0:T(8,128)(2,1)S(1)} %shard_map.78.refs_0_, bf16[2,3,64,512]{3,2,1,0:T(8,128)(2,1)S(1)} %collective-permute-done.2.refs_1_, ...), custom_call_target="tpu_custom_call" | custom-call | flops 4718592 | bytes 1179648 | tf_op jit(solution)/shard_map/cross_last/pallas_call | solution.py:293
  68.1 1.6 %collective-permute-start.11 = (bf16[104,256]{1,0:T(8,128)(2,1)S(1)}, bf16[104,256]{1,0:T(8,128)(2,1)S(1)}, u32[]{:S(2)}, u32[]{:S(2)}) collective-permute-start(bf16[104,256]{1,0:T(8,128)(2,1)S(1)} %get-tuple-element.28), channel_id=1, source_target_pairs={{0,16},{1,17},{2,18},{3,19},{4,20},{5,21},{6,22},{7,23},{24,8},{25... | collective-permute-start | bytes 159752 | tf_op jit(solution)/shard_map/ppermute | solution.py:385
  69.7 1.8 %collective-permute-done.11.from_y = bf16[104,256]{1,0:T(8,128)(2,1)S(1)} collective-permute-done((bf16[104,256]{1,0:T(8,128)(2,1)S(1)}, bf16[104,256]{1,0:T(8,128)(2,1)S(1)}, u32[]{:S(2)}, u32[]{:S(2)}) %collective-permute-start.11) | collective-permute-done | bytes 53280 | tf_op jit(solution)/shard_map/ppermute | solution.py:385
  72.1 7.0 %collective-permute-start.12 = (bf16[104,256]{1,0:T(8,128)(2,1)S(1)}, bf16[104,256]{1,0:T(8,128)(2,1)S(1)}, u32[]{:S(2)}, u32[]{:S(2)}) collective-permute-start(bf16[104,256]{1,0:T(8,128)(2,1)S(1)} %get-tuple-element.30), channel_id=1, source_target_pairs={{0,8},{1,9},{2,10},{3,11},{4,12},{5,13},{6,14},{7,15},{8,0},{9,1},... | collective-permute-start | bytes 159752 | tf_op jit(solution)/shard_map/ppermute | solution.py:385
  79.1 0.9 collective-permute-done.12.got
  80.6 0.8 collective-permute-start.13
  81.4 4.5 %collective-permute-done.13 = bf16[104,512]{1,0:T(8,128)(2,1)S(1)} collective-permute-done((bf16[104,512]{1,0:T(8,128)(2,1)S(1)}, bf16[104,512]{1,0:T(8,128)(2,1)S(1)}, u32[]{:S(2)}, u32[]{:S(2)}) %collective-permute-start.13) | collective-permute-done | bytes 106528 | tf_op jit(solution)/shard_map/ppermute | solution.py:385
  86.0 1.6 %collective-permute-start.14 = (bf16[104,512]{1,0:T(8,128)(2,1)S(1)}, bf16[104,512]{1,0:T(8,128)(2,1)S(1)}, u32[]{:S(2)}, u32[]{:S(2)}) collective-permute-start(bf16[104,512]{1,0:T(8,128)(2,1)S(1)} %add_convert_fusion.1), channel_id=1, source_target_pairs={{0,1},{1,0},{2,3},{3,2},{4,5},{5,4},{6,7},{7,6},{8,9},{9,8},{10,11... | collective-permute-start | bytes 319496 | tf_op jit(solution)/shard_map/ppermute | solution.py:385
  87.6 3.2 %collective-permute-done.14 = bf16[104,512]{1,0:T(8,128)(2,1)S(1)} collective-permute-done((bf16[104,512]{1,0:T(8,128)(2,1)S(1)}, bf16[104,512]{1,0:T(8,128)(2,1)S(1)}, u32[]{:S(2)}, u32[]{:S(2)}) %collective-permute-start.14) | collective-permute-done | bytes 106528 | tf_op jit(solution)/shard_map/ppermute | solution.py:385
  90.8 3.1 %collective-permute-start.15 = (bf16[104,512]{1,0:T(8,128)(2,1)S(1)}, bf16[104,512]{1,0:T(8,128)(2,1)S(1)}, u32[]{:S(2)}, u32[]{:S(2)}) collective-permute-start(bf16[104,512]{1,0:T(8,128)(2,1)S(1)} %add_convert_fusion), channel_id=1, source_target_pairs={{0,2},{1,3},{2,0},{3,1},{4,6},{5,7},{6,4},{7,5},{8,10},{9,11},{10,... | collective-permute-start | bytes 319496 | tf_op jit(solution)/shard_map/ppermute | solution.py:385
  93.9 3.2 %collective-permute-done.15 = bf16[104,512]{1,0:T(8,128)(2,1)S(1)} collective-permute-done((bf16[104,512]{1,0:T(8,128)(2,1)S(1)}, bf16[104,512]{1,0:T(8,128)(2,1)S(1)}, u32[]{:S(2)}, u32[]{:S(2)}) %collective-permute-start.15) | collective-permute-done | bytes 106528 | tf_op jit(solution)/shard_map/ppermute | solution.py:385
  97.1 0.7 reshape.5
  (31 shorter events, 2.8 us)
Async XLA Ops:
  0.0 2.8 %copy-start = (bf16[1,24,128,1024]{3,2,1,0:T(8,128)(2,1)S(1)}, bf16[1,24,128,1024]{3,2,1,0:T(8,128)(2,1)}, u32[]{:S(2)}) copy-start(bf16[1,24,128,1024]{3,2,1,0:T(8,128)(2,1)} %param.7) | copy-start | bytes 18874372
  2.8 0.9 copy-start.3
  4.8 5.8 %copy-start.1 = (bf16[1024,512]{1,0:T(8,128)(2,1)S(1)}, bf16[1024,512]{1,0:T(8,128)(2,1)}, u32[]{:S(2)}) copy-start(bf16[1024,512]{1,0:T(8,128)(2,1)} %constant.43.clone.forward) | copy-start | bytes 3145732
  4.8 5.8 %copy-start.2 = (bf16[512,256]{1,0:T(8,128)(2,1)S(1)}, bf16[512,256]{1,0:T(8,128)(2,1)}, u32[]{:S(2)}) copy-start(bf16[512,256]{1,0:T(8,128)(2,1)} %constant.44.clone.band) | copy-start | bytes 786436
  4.8 12.1 %collective-permute-start.1 = (bf16[18,64,1024]{2,1,0:T(8,128)(2,1)S(1)}, bf16[18,64,1024]{2,1,0:T(8,128)(2,1)S(1)}, u32[]{:S(2)}, u32[]{:S(2)}) collective-permute-start(bf16[18,64,1024]{2,1,0:T(8,128)(2,1)S(1)} %shard_map.75), channel_id=1, source_target_pairs={{0,8},{1,9},{2,10},{3,11},{4,12},{5,13},{6,14},{7,15},{8,0},{9,1},... | collective-permute-start | bytes 7077896 | tf_op jit(solution)/shard_map/ppermute | solution.py:385
  5.7 4.9 %collective-permute-start = (bf16[6,64,1024]{2,1,0:T(8,128)(2,1)S(1)}, bf16[6,64,1024]{2,1,0:T(8,128)(2,1)S(1)}, u32[]{:S(2)}, u32[]{:S(2)}) collective-permute-start(bf16[6,64,1024]{2,1,0:T(8,128)(2,1)S(1)} %shard_map.73), channel_id=1, source_target_pairs={{0,8},{1,9},{2,10},{3,11},{4,12},{5,13},{6,14},{7,15},{8,0},{9,1},... | collective-permute-start | bytes 2359304 | tf_op jit(solution)/shard_map/ppermute | solution.py:385
  13.2 16.7 %collective-permute-start.6 = (bf16[2,6,64,512]{3,2,1,0:T(8,128)(2,1)S(1)}, bf16[2,6,64,512]{3,2,1,0:T(8,128)(2,1)S(1)}, u32[]{:S(2)}, u32[]{:S(2)}) collective-permute-start(bf16[2,6,64,512]{3,2,1,0:T(8,128)(2,1)S(1)} %shard_map.74.refs_0_), channel_id=1, source_target_pairs={{8,40},{9,41},{10,42},{11,43},{12,44},{13,45},{14,46},{15,47},{24,... | collective-permute-start | bytes 2359304 | tf_op jit(solution)/shard_map/ppermute | solution.py:385
  20.6 31.9 %collective-permute-start.8 = (bf16[2,9,64,512]{3,2,1,0:T(8,128)(2,1)S(1)}, bf16[2,9,64,512]{3,2,1,0:T(8,128)(2,1)S(1)}, u32[]{:S(2)}, u32[]{:S(2)}) collective-permute-start(bf16[2,9,64,512]{3,2,1,0:T(8,128)(2,1)S(1)} %shard_map.76.refs_3_), channel_id=1, source_target_pairs={{8,40},{9,41},{10,42},{11,43},{12,44},{13,45},{14,46},{15,47},{24,... | collective-permute-start | bytes 3538952 | tf_op jit(solution)/shard_map/ppermute | solution.py:385
  22.5 31.3 %collective-permute-start.9 = (bf16[2,9,64,512]{3,2,1,0:T(8,128)(2,1)S(1)}, bf16[2,9,64,512]{3,2,1,0:T(8,128)(2,1)S(1)}, u32[]{:S(2)}, u32[]{:S(2)}) collective-permute-start(bf16[2,9,64,512]{3,2,1,0:T(8,128)(2,1)S(1)} %shard_map.76.refs_3_), channel_id=1, source_target_pairs={{8,24},{9,25},{10,26},{11,27},{12,28},{13,29},{14,30},{15,31},{16,... | collective-permute-start | bytes 3538952 | tf_op jit(solution)/shard_map/ppermute | solution.py:385
  23.8 26.7 %collective-permute-start.7 = (bf16[2,6,64,512]{3,2,1,0:T(8,128)(2,1)S(1)}, bf16[2,6,64,512]{3,2,1,0:T(8,128)(2,1)S(1)}, u32[]{:S(2)}, u32[]{:S(2)}) collective-permute-start(bf16[2,6,64,512]{3,2,1,0:T(8,128)(2,1)S(1)} %shard_map.74.refs_0_), channel_id=1, source_target_pairs={{8,24},{9,25},{10,26},{11,27},{12,28},{13,29},{14,30},{15,31},{16,... | collective-permute-start | bytes 2359304 | tf_op jit(solution)/shard_map/ppermute | solution.py:385
  27.8 26.0 %copy-start.4 = (bf16[112,512]{1,0:T(8,128)(2,1)S(1)}, bf16[112,512]{1,0:T(8,128)(2,1)}, u32[]{:S(2)}) copy-start(bf16[112,512]{1,0:T(8,128)(2,1)} %constant.45.clone.refs_6_.refs_4_) | copy-start | bytes 344068
  27.8 26.0 %copy-start.5 = (bf16[112,512]{1,0:T(8,128)(2,1)S(1)}, bf16[112,512]{1,0:T(8,128)(2,1)}, u32[]{:S(2)}) copy-start(bf16[112,512]{1,0:T(8,128)(2,1)} %constant.46.clone.refs_7_.refs_5_) | copy-start | bytes 344068
  27.8 33.0 %collective-permute-start.4 = (bf16[2,6,64,512]{3,2,1,0:T(8,128)(2,1)S(1)}, bf16[2,6,64,512]{3,2,1,0:T(8,128)(2,1)S(1)}, u32[]{:S(2)}, u32[]{:S(2)}) collective-permute-start(bf16[2,6,64,512]{3,2,1,0:T(8,128)(2,1)S(1)} %shard_map.77.refs_0_), channel_id=1, source_target_pairs={{8,40},{9,41},{10,42},{11,43},{12,44},{13,45},{14,46},{15,47},{24,... | collective-permute-start | bytes 2359304 | tf_op jit(solution)/shard_map/ppermute | solution.py:385
  29.9 30.9 %collective-permute-start.5 = (bf16[2,6,64,512]{3,2,1,0:T(8,128)(2,1)S(1)}, bf16[2,6,64,512]{3,2,1,0:T(8,128)(2,1)S(1)}, u32[]{:S(2)}, u32[]{:S(2)}) collective-permute-start(bf16[2,6,64,512]{3,2,1,0:T(8,128)(2,1)S(1)} %shard_map.77.refs_0_), channel_id=1, source_target_pairs={{8,24},{9,25},{10,26},{11,27},{12,28},{13,29},{14,30},{15,31},{16,... | collective-permute-start | bytes 2359304 | tf_op jit(solution)/shard_map/ppermute | solution.py:385
  50.6 14.1 %collective-permute-start.2 = (bf16[2,3,64,512]{3,2,1,0:T(8,128)(2,1)S(1)}, bf16[2,3,64,512]{3,2,1,0:T(8,128)(2,1)S(1)}, u32[]{:S(2)}, u32[]{:S(2)}) collective-permute-start(bf16[2,3,64,512]{3,2,1,0:T(8,128)(2,1)S(1)} %shard_map.78.refs_0_), channel_id=1, source_target_pairs={{8,40},{9,41},{10,42},{11,43},{12,44},{13,45},{14,46},{15,47},{24,... | collective-permute-start | bytes 1179656 | tf_op jit(solution)/shard_map/ppermute | solution.py:385
  52.5 12.2 %collective-permute-start.3 = (bf16[2,3,64,512]{3,2,1,0:T(8,128)(2,1)S(1)}, bf16[2,3,64,512]{3,2,1,0:T(8,128)(2,1)S(1)}, u32[]{:S(2)}, u32[]{:S(2)}) collective-permute-start(bf16[2,3,64,512]{3,2,1,0:T(8,128)(2,1)S(1)} %shard_map.78.refs_0_), channel_id=1, source_target_pairs={{8,24},{9,25},{10,26},{11,27},{12,28},{13,29},{14,30},{15,31},{16,... | collective-permute-start | bytes 1179656 | tf_op jit(solution)/shard_map/ppermute | solution.py:385
  60.8 18.3 %copy-start.6 = (s32[1,4]{1,0:T(1,128)S(1)}, s32[1,4]{1,0:T(1,128)}, u32[]{:S(2)}) copy-start(s32[1,4]{1,0:T(1,128)} %param.9) | copy-start | bytes 52
  67.4 4.0 %collective-permute-start.10 = (bf16[104,512]{1,0:T(8,128)(2,1)S(1)}, bf16[104,512]{1,0:T(8,128)(2,1)S(1)}, u32[]{:S(2)}, u32[]{:S(2)}) collective-permute-start(bf16[104,512]{1,0:T(8,128)(2,1)S(1)} %get-tuple-element.27), channel_id=1, source_target_pairs={{40,8},{41,9},{42,10},{43,11},{44,12},{45,13},{46,14},{47,15},{56,... | collective-permute-start | bytes 319496 | tf_op jit(solution)/shard_map/ppermute | solution.py:385
  68.1 3.3 %collective-permute-start.11 = (bf16[104,256]{1,0:T(8,128)(2,1)S(1)}, bf16[104,256]{1,0:T(8,128)(2,1)S(1)}, u32[]{:S(2)}, u32[]{:S(2)}) collective-permute-start(bf16[104,256]{1,0:T(8,128)(2,1)S(1)} %get-tuple-element.28), channel_id=1, source_target_pairs={{0,16},{1,17},{2,18},{3,19},{4,20},{5,21},{6,22},{7,23},{24,8},{25... | collective-permute-start | bytes 159752 | tf_op jit(solution)/shard_map/ppermute | solution.py:385
  72.1 7.9 %collective-permute-start.12 = (bf16[104,256]{1,0:T(8,128)(2,1)S(1)}, bf16[104,256]{1,0:T(8,128)(2,1)S(1)}, u32[]{:S(2)}, u32[]{:S(2)}) collective-permute-start(bf16[104,256]{1,0:T(8,128)(2,1)S(1)} %get-tuple-element.30), channel_id=1, source_target_pairs={{0,8},{1,9},{2,10},{3,11},{4,12},{5,13},{6,14},{7,15},{8,0},{9,1},... | collective-permute-start | bytes 159752 | tf_op jit(solution)/shard_map/ppermute | solution.py:385
  80.6 5.3 %collective-permute-start.13 = (bf16[104,512]{1,0:T(8,128)(2,1)S(1)}, bf16[104,512]{1,0:T(8,128)(2,1)S(1)}, u32[]{:S(2)}, u32[]{:S(2)}) collective-permute-start(bf16[104,512]{1,0:T(8,128)(2,1)S(1)} %assemble.1), channel_id=1, source_target_pairs={{0,4},{1,5},{2,6},{3,7},{4,0},{5,1},{6,2},{7,3},{8,12},{9,13},{10,... | collective-permute-start | bytes 319496 | tf_op jit(solution)/shard_map/ppermute | solution.py:385
  86.0 4.8 %collective-permute-start.14 = (bf16[104,512]{1,0:T(8,128)(2,1)S(1)}, bf16[104,512]{1,0:T(8,128)(2,1)S(1)}, u32[]{:S(2)}, u32[]{:S(2)}) collective-permute-start(bf16[104,512]{1,0:T(8,128)(2,1)S(1)} %add_convert_fusion.1), channel_id=1, source_target_pairs={{0,1},{1,0},{2,3},{3,2},{4,5},{5,4},{6,7},{7,6},{8,9},{9,8},{10,11... | collective-permute-start | bytes 319496 | tf_op jit(solution)/shard_map/ppermute | solution.py:385
  90.8 6.3 %collective-permute-start.15 = (bf16[104,512]{1,0:T(8,128)(2,1)S(1)}, bf16[104,512]{1,0:T(8,128)(2,1)S(1)}, u32[]{:S(2)}, u32[]{:S(2)}) collective-permute-start(bf16[104,512]{1,0:T(8,128)(2,1)S(1)} %add_convert_fusion), channel_id=1, source_target_pairs={{0,2},{1,3},{2,0},{3,1},{4,6},{5,7},{6,4},{7,5},{8,10},{9,11},{10,... | collective-permute-start | bytes 319496 | tf_op jit(solution)/shard_map/ppermute | solution.py:385
where the time goes:
time: 98.3 us; the launch traced here: 97.9 us
  waiting for transfers between devices  35.8 us (36%)
  starting transfers between devices  30.2 us (31%)
  Pallas kernels  27.1 us (28%)
  local copies, waits for them, and re-layouts  4.46 us (5%)
    ppermute x16, waiting for transfers between devices, move(): return lax.ppermute(block, ('chan', 'tm'), route(blocks, times, target))  35.8 us
    ppermute x16, starting transfers between devices, move(): return lax.ppermute(block, ('chan', 'tm'), route(blocks, times, target))  30.2 us
    pallas_call x3, Pallas kernels, cross(): pl.pallas_call(functools.partial(cross_kernel, counts, start, last), grid...  13.5 us
    pallas_call x4, Pallas kernels, whiten(): pl.pallas_call(functools.partial(whiten_kernel, first), grid_spec=pltpu.P...  10.4 us
    unnamed x14, local copies, waits for them, and re-layouts  3.71 us
  transfers between devices with their start and end apart: 16, of which 7 were waited for; matrix products, arithmetic and copies ran while one was open for 0% of the time, Pallas kernels for 22%

commit v1 on v0

v1 whole, which is shorter than its diff:
```python
import functools
import math

import jax
import jax.numpy as jnp
import numpy as np
from jax import lax
from jax.experimental import pallas as pl
from jax.experimental.pallas import tpu as pltpu
from jax.sharding import PartitionSpec as P

NF = 256
WIN = 1024
MAXLAG = 50
SMOOTH = 4
REACH = 4
LAGS = 2 * MAXLAG + 1
ROWS = 104
TABLE_ROWS = 112
HALF = 64
STEP = 3
TILE = 16
PLANES = 12
CHUNKS = ((0, 6), (6, 9), (15, 6), (21, 3))
VMEM = 24 << 20
WATER = 0.05
EPS = 1e-06


f32 = jnp.float32
bf16 = jnp.bfloat16


def forward_table():
    samples = np.arange(WIN, dtype=np.int32)
    bins = np.arange(1, NF + 1, dtype=np.int32)
    phase = samples[:, None] * bins[None, :] % WIN
    angle = phase.astype(np.float32) * np.float32(2.0 * math.pi / WIN)
    return np.concatenate([np.cos(angle), -np.sin(angle)], axis=1).astype(bf16)


def inverse_tables(windows_all):
    bins = np.arange(1, NF + 1, dtype=np.int32)
    offsets = np.arange(LAGS, dtype=np.int32) - MAXLAG
    phase = bins[None, :] * offsets[:, None] % WIN
    angle = phase.astype(np.float32) * np.float32(2.0 * math.pi / WIN)
    factor = np.float32(1.0 / math.sqrt(windows_all * NF))
    table = np.concatenate([np.cos(angle), -np.sin(angle)], axis=1) * factor
    table = np.pad(table, ((0, TABLE_ROWS - LAGS), (0, 0))).astype(np.float32)
    high = table.astype(bf16)
    low = (table - high.astype(np.float32)).astype(bf16)
    return high, low


def band_table():
    bins = np.arange(NF)
    near = np.abs(bins[:, None] - bins[None, :]) <= SMOOTH
    return np.concatenate([near, near], axis=0).astype(bf16)


def prepare_kernel(first, role, traces, mask, own, give):
    i = pl.program_id(0)
    core = role[1]
    for j in range(STEP):
        keep = mask[pl.ds(first + i * STEP + j, 1), :].astype(bf16)
        own[j] = traces[j, pl.ds(pl.multiple_of(core * HALF, HALF), HALF), :] * keep
        give[j] = traces[j, pl.ds(pl.multiple_of((1 - core) * HALF, HALF), HALF), :] * keep


def prepare(role, traces, mask, first, count):
    base = first // STEP
    block = pl.BlockSpec((STEP, HALF, WIN), lambda i, role: (i, 0, 0))
    part = jax.ShapeDtypeStruct((count, HALF, WIN), bf16)
    return pl.pallas_call(
        functools.partial(prepare_kernel, first),
        grid_spec=pltpu.PrefetchScalarGridSpec(
            num_scalar_prefetch=1,
            grid=(count // STEP,),
            in_specs=[
                pl.BlockSpec((STEP, 2 * HALF, WIN), lambda i, role: (base + i, 0, 0)),
                pl.BlockSpec(mask.shape, lambda i, role: (0, 0)),
            ],
            out_specs=[block, block],
        ),
        out_shape=[part, part],
        compiler_params=pltpu.CompilerParams(vmem_limit_bytes=VMEM),
        cost_estimate=pl.CostEstimate(
            flops=2 * count * HALF * WIN, bytes_accessed=8 * count * HALF * WIN, transcendentals=0
        ),
    )(role, traces, mask)


def whiten_kernel(role, kept, given, forward, band, out, spectra, split, level):
    core = role[1]
    part = STEP * HALF
    spectra[:part] = jnp.dot(kept[...].reshape(part, WIN), forward[...], preferred_element_type=f32)
    spectra[part:] = jnp.dot(given[...].reshape(part, WIN), forward[...], preferred_element_type=f32)
    for r in range(0, 2 * STEP * HALF, 32):
        rows = slice(r, r + 32)
        real = spectra[rows, :NF]
        imag = spectra[rows, NF:]
        amplitude = jnp.sqrt(real * real + imag * imag)
        high = amplitude.astype(bf16)
        split[rows, :NF] = high
        split[rows, NF:] = (amplitude - high.astype(f32)).astype(bf16)
        total = jnp.sum(amplitude, axis=-1, keepdims=True)
        level[rows, :] = jnp.broadcast_to(total * f32(WATER / NF) + f32(EPS), (32, 128))
    smooth = jnp.dot(split[...], band[...], preferred_element_type=f32)
    for r in range(0, 2 * STEP * HALF, 32):
        rows = slice(r, r + 32)
        base = level[rows, :]
        divisor = smooth[rows, :] * f32(1.0 / (2 * SMOOTH + 1)) + jnp.concatenate([base, base], axis=1)
        inverse = 1.0 / divisor
        h, rest = divmod(r, STEP * HALF)
        j, c = divmod(rest, HALF)
        block = core if h == 0 else 1 - core
        out[block, j, c : c + 32, :NF] = (spectra[rows, :NF] * inverse).astype(bf16)
        out[block, j, c : c + 32, NF:] = (spectra[rows, NF:] * inverse).astype(bf16)


def whiten(role, kept, given, forward, band, count, skip):
    rows = 2 * STEP * HALF
    skip = skip // STEP
    return pl.pallas_call(
        whiten_kernel,
        grid_spec=pltpu.PrefetchScalarGridSpec(
            num_scalar_prefetch=1,
            grid=(count // STEP,),
            in_specs=[
                pl.BlockSpec((STEP, HALF, WIN), lambda i, role: (skip + i, 0, 0)),
                pl.BlockSpec((STEP, HALF, WIN), lambda i, role: (skip + i, 0, 0)),
                pl.BlockSpec(forward.shape, lambda i, role: (0, 0)),
                pl.BlockSpec(band.shape, lambda i, role: (0, 0)),
            ],
            out_specs=pl.BlockSpec((2, STEP, HALF, 2 * NF), lambda i, role: (0, i, 0, 0)),
            scratch_shapes=[
                pltpu.VMEM((rows, 2 * NF), f32),
                pltpu.VMEM((rows, 2 * NF), bf16),
                pltpu.VMEM((rows, 128), f32),
            ],
        ),
        out_shape=jax.ShapeDtypeStruct((2, count, HALF, 2 * NF), bf16),
        compiler_params=pltpu.CompilerParams(vmem_limit_bytes=VMEM),
        cost_estimate=pl.CostEstimate(
            flops=2 * count * 2 * HALF * (WIN * 2 * NF + 2 * NF * NF),
            bytes_accessed=count * 2 * HALF * (WIN + 2 * NF) * 2,
            transcendentals=count * 2 * HALF * NF * 2,
        ),
    )(role, kept, given, forward, band)


def cross_kernel(start, last, role, own, near, across, *refs):
    before = None
    if not start:
        before, refs = refs[0], refs[1:]
    table_high, table_low, *refs = refs
    if last:
        kept, to_z, to_y, total = refs
    else:
        kept, total = refs
    y_hi = role[0]
    core = role[1]
    count = own.shape[1]
    zero = jnp.zeros((TILE, 128), f32)

    def tile(t, carry):
        rows = pl.ds(pl.multiple_of(t * TILE, TILE), TILE)
        for f in range(0, NF, 128):
            re = slice(f, f + 128)
            im = slice(NF + f, NF + f + 128)

            def run(blocks, pairs):
                used = sorted({s for _, a, b in pairs for s in (a, b)})

                def window(w, sums):
                    at = {}
                    for s in used:
                        ref = blocks[s // 2]
                        at[s] = (ref[s % 2, w, rows, re].astype(f32), ref[s % 2, w, rows, im].astype(f32))
                    out = []
                    for (_, a, b), (sr, si) in zip(pairs, sums):
                        ar, ai = at[a]
                        br, bi = at[b]
                        out.append((sr + (ar * br + ai * bi), si + (ar * bi - ai * br)))
                    return tuple(out)

                sums = lax.fori_loop(0, count, window, tuple((zero, zero) for _ in pairs), unroll=3)
                for (plane, _, _), (sr, si) in zip(pairs, sums):
                    total[plane, rows, re] = sr
                    total[plane, rows, im] = si

            inner = ((3, 0, 2), (6, 1, 2), (7, 1, 3))

            def all_pairs(blocks, local):
                run(blocks, (local, *inner))

                @pl.when(y_hi == core)
                def _():
                    run(blocks, ((1, 0, 4), (2, 0, 5), (4, 1, 4), (5, 1, 5)))
                    run(blocks, ((8, 4, 2), (9, 4, 3), (10, 5, 2), (11, 5, 3)))

            @pl.when(core == 0)
            def _():
                all_pairs((own, near, across), (0, 0, 1))

            @pl.when(core != 0)
            def _():
                all_pairs((near, own, across), (0, 2, 3))

            @pl.when(y_hi != core)
            def _():
                for plane in (1, 2, 4, 5, 8, 9, 10, 11):
                    total[plane, rows, re] = zero
                    total[plane, rows, im] = zero

        return carry

    lax.fori_loop(0, HALF // TILE, tile, 0)
    stack = total[...].reshape(PLANES * HALF, 2 * NF)
    high = stack.astype(bf16)
    dims = (((1,), (1,)), ((), ()))
    dot = functools.partial(lax.dot_general, dimension_numbers=dims, preferred_element_type=f32)
    result = dot(table_high[...], high)
    if not last:
        low = (stack - high.astype(f32)).astype(bf16)
        result = result + (dot(table_high[...], low) + dot(table_low[...], high))
    result = result[:ROWS]
    if not start:
        result = result + before[...]
    if not last:
        kept[...] = result
        return
    near_part = result[:, : 8 * HALF]
    lane = lax.broadcasted_iota(jnp.int32, near_part.shape, 1)
    kept[...] = jnp.where((lane < jnp.where(core == 0, 8 * HALF, HALF)), near_part, 0.0)
    to_z[...] = jnp.where(lane < HALF, 0.0, near_part).astype(bf16)
    to_y[...] = result[:, 8 * HALF :].astype(bf16)


def whole(shape):
    return pl.BlockSpec(shape, lambda i, role: (0,) * len(shape))


def cross(role, operands, before, tables, last):
    start = before is None
    count = operands[0].shape[1]
    args = [role, *operands]
    if not start:
        args.append(before)
    args += list(tables)
    in_vmem = pl.BlockSpec(memory_space=pltpu.VMEM)
    if last:
        out_shape = [
            jax.ShapeDtypeStruct((ROWS, 8 * HALF), f32),
            jax.ShapeDtypeStruct((ROWS, 8 * HALF), bf16),
            jax.ShapeDtypeStruct((ROWS, 4 * HALF), bf16),
        ]
        out_specs = [in_vmem] * 3
    else:
        out_shape = jax.ShapeDtypeStruct((ROWS, PLANES * HALF), f32)
        out_specs = in_vmem
    return pl.pallas_call(
        functools.partial(cross_kernel, start, last),
        in_specs=[pl.BlockSpec(memory_space=pltpu.SMEM)] + [in_vmem] * (len(args) - 1),
        out_specs=out_specs,
        out_shape=out_shape,
        scratch_shapes=[pltpu.VMEM((PLANES, HALF, 2 * NF), f32)],
        compiler_params=pltpu.CompilerParams(vmem_limit_bytes=VMEM),
        cost_estimate=pl.CostEstimate(
            flops=PLANES * 8 * count * HALF * NF,
            bytes_accessed=6 * count * HALF * 2 * NF * 2,
            transcendentals=0,
        ),
    )(*args)


def combine_kernel(role, kept, from_z, from_y, own, give):
    core = role[1]
    y = jnp.where(role[0] != core, from_y[...].astype(f32), 0.0)
    z = jnp.where((core != 0) & (role[2] == 0), from_z[...].astype(f32), 0.0)
    gap = jnp.zeros((ROWS, HALF), f32)
    placed = jnp.concatenate([gap, y[:, : 2 * HALF], gap, y[:, 2 * HALF :], gap, gap], axis=1)
    total = (kept[...] + z + placed).astype(bf16)
    first, second = total[:, : 4 * HALF].astype(f32), total[:, 4 * HALF :].astype(f32)
    own[...] = jnp.where(core == 0, first, second).astype(bf16)
    give[...] = jnp.where(core == 0, second, first).astype(bf16)


def combine(role, kept, from_z, from_y):
    part = jax.ShapeDtypeStruct((ROWS, 4 * HALF), bf16)
    return pl.pallas_call(
        combine_kernel,
        grid_spec=pltpu.PrefetchScalarGridSpec(
            num_scalar_prefetch=1,
            grid=(1,),
            in_specs=[whole(a.shape) for a in (kept, from_z, from_y)],
            out_specs=[whole(part.shape)] * 2,
        ),
        out_shape=[part, part],
        compiler_params=pltpu.CompilerParams(vmem_limit_bytes=VMEM),
        name="combine",
    )(role, kept, from_z, from_y)


def assemble_kernel(role, slots, own, got, out):
    core = role[1]
    mine, other = own[...].astype(f32), got[...].astype(f32)
    first = jnp.where(core == 0, mine, other)
    second = jnp.where(core == 0, other, mine)
    planes = [
        jnp.concatenate([first[:, i * HALF : (i + 1) * HALF], second[:, i * HALF : (i + 1) * HALF]], axis=1)
        for i in range(REACH)
    ]
    for slot in range(REACH):
        distance = slots[slot]
        value = jnp.zeros((ROWS, 2 * HALF), f32)
        for k in range(REACH):
            value = jnp.where(distance == k + 1, planes[k], value)
        out[:, slot * 2 * HALF : (slot + 1) * 2 * HALF] = value.astype(bf16)


def assemble(role, slots, own, got):
    shape = (ROWS, REACH * 2 * HALF)
    return pl.pallas_call(
        assemble_kernel,
        grid_spec=pltpu.PrefetchScalarGridSpec(
            num_scalar_prefetch=2,
            grid=(1,),
            in_specs=[pl.BlockSpec(own.shape, lambda i, *_: (0, 0)), pl.BlockSpec(got.shape, lambda i, *_: (0, 0))],
            out_specs=pl.BlockSpec(shape, lambda i, *_: (0, 0)),
        ),
        out_shape=jax.ShapeDtypeStruct(shape, bf16),
        compiler_params=pltpu.CompilerParams(vmem_limit_bytes=VMEM),
        name="assemble",
    )(role, slots, own, got)


def route(blocks, times, target):
    pairs = []
    for b in range(blocks):
        z, y_hi, core = b // 4, b // 2 % 2, b % 2
        for t in range(times):
            to_z, to_y, to_core, to_t = target(z, y_hi, core, t)
            if not 0 <= to_z < blocks // 4:
                to_z, to_core = z, 1 - core
            pairs.append((b * times + t, ((to_z * 2 + to_y) * 2 + to_core) * times + to_t))
    return pairs


def body(traces, valid_mask, pair_owner):
    blocks, times = lax.axis_size("chan"), lax.axis_size("tm")
    windows_all = traces.shape[1] * times

    def move(block, target):
        return lax.ppermute(block, ("chan", "tm"), route(blocks, times, target))

    def to_core(block):
        return move(block, lambda z, y, c, t: (z, y, 1 - c, t))

    reader = lax.axis_index("chan")
    core = reader % 2
    top = (reader // 4 == blocks // 4 - 1).astype(jnp.int32)
    places = jnp.arange(3, dtype=jnp.int32)
    role = jnp.where(places == 0, reader // 2 % 2, jnp.where(places == 1, core, top))
    slots = pair_owner[0] - reader
    forward, band = jnp.asarray(forward_table()), jnp.asarray(band_table())
    high, low = inverse_tables(windows_all)
    tables = (jnp.asarray(high), jnp.asarray(low))
    mask = valid_mask[0].astype(f32)

    rest = CHUNKS[0][1]
    later = traces.shape[1] - rest
    head, give = prepare(role, traces[0], mask, 0, rest)
    given_head = to_core(give)
    tail, give = prepare(role, traces[0], mask, rest, later)
    given_tail = to_core(give)
    sets = []
    order = role
    for k, (first, count) in enumerate(CHUNKS):
        if k == 0:
            own = whiten(order, head, given_head, forward, band, count, 0)
        else:
            own = whiten(order, tail, given_tail, forward, band, count, first - rest)
        own, order = lax.optimization_barrier((own, order))
        near = move(own, lambda z, y, c, t: (z - 1 + 2 * c, y, c, t))
        across = move(own, lambda z, y, c, t: (z, 1 - y, c, t) if y != c else (z, y, 1 - c, t))
        sets.append((own, near, across))
    stack = None
    for k, operands in enumerate(sets):
        stack = cross(order, operands, stack, tables, k == len(sets) - 1)
    kept, for_z, for_y = stack
    from_z = move(for_z, lambda z, y, c, t: (z + 1 - 2 * c, y, c, t))
    from_y = move(for_y, lambda z, y, c, t: (z, 1 - y, c, t) if y == c else (z, y, 1 - c, t))
    mine, give = combine(role, kept, from_z, from_y)
    partial = assemble(role, slots, mine, to_core(give))

    def exchange(block, bit):
        return move(block, lambda z, y, c, t: (z, y, c, t ^ bit)).astype(f32)

    partial = (partial.astype(f32) + exchange(partial, 4)).astype(bf16)
    far, third, near = (exchange(partial, bit) for bit in (2, 3, 1))
    partial = (partial.astype(f32) + near) + (far + third)
    result = partial[:LAGS].reshape(LAGS, REACH, 2 * HALF)
    return result.transpose(1, 0, 2)[None]


def solution(mesh):
    return jax.shard_map(
        body,
        mesh=mesh,
        in_specs=(P("chan", "tm", None, None), P("chan", "tm", None), P("chan", None)),
        out_specs=P("chan", None, None, None),
        check_vma=False,
    )
```

time: 98.3 us -> 84 us (0.85)
  starting transfers between devices: 30.2 us -> 19.6 us
  Pallas kernels: 27.1 us -> 24.6 us
    ppermute x16 -> x17, starting transfers between devices: 30.2 us -> 19.6 us  [move(): return lax.ppermute(block, ('chan', 'tm'), route(blocks, times, target))]
    pallas_call x9 -> x10, Pallas kernels: 25.8 us -> 23.3 us  [the longest x4 12.9 us: cross(): pl.pallas_call(functools.partial(cross_kernel, start, last), in_specs=[pl...]
    unnamed x14 -> x12, local copies, waits for them, and re-layouts: 3.71 us -> 2.81 us
    ppermute x16 -> x17, waiting for transfers between devices: 35.8 us -> 35 us  [move(): return lax.ppermute(block, ('chan', 'tm'), route(blocks, times, target))]
  transfers between devices with their start and end apart: 16 -> 17, of which waited for: 7 -> 10; matrix products, arithmetic and copies ran while one was open for 0% -> 0% of each run, Pallas kernels for 22% -> 24%
where the time goes in v1:
time: 84 us; the launch traced here: 83.9 us
  waiting for transfers between devices  35 us (42%)
  Pallas kernels  24.6 us (29%)
  starting transfers between devices  19.6 us (23%)
  local copies, waits for them, and re-layouts  3.56 us (4%)
  other arithmetic  0.99 us (1%)
    ppermute x17, waiting for transfers between devices, move(): return lax.ppermute(block, ('chan', 'tm'), route(blocks, times, target))  35 us
    ppermute x17, starting transfers between devices, move(): return lax.ppermute(block, ('chan', 'tm'), route(blocks, times, target))  19.6 us
    pallas_call x4, Pallas kernels, cross(): pl.pallas_call(functools.partial(cross_kernel, start, last), in_specs=[pl...  12.9 us
    pallas_call x4, Pallas kernels, whiten(): pl.pallas_call(whiten_kernel, grid_spec=pltpu.PrefetchScalarGridSpec(num_...  8.69 us
    unnamed x12, local copies, waits for them, and re-layouts  2.81 us
    pallas_call x2, Pallas kernels, prepare(): pl.pallas_call(functools.partial(prepare_kernel, first), grid_spec=pltpu....  1.74 us
  transfers between devices with their start and end apart: 17, of which 10 were waited for; matrix products, arithmetic and copies ran while one was open for 0% of the time, Pallas kernels for 24%

profile of v1, /device:TPU:32, one launch (start us, length us, event | category | flops | bytes accessed | tf_op | source)
XLA Modules:
  0.0 83.9 jit_solution(6477721109323351323)
XLA Ops:
  0.0 0.9 %convert_bitcast_fusion.mask = f32[24,1024]{1,0:T(8,128)S(1)} fusion(s32[1,24,1024]{2,1,0:T(8,128)} %param.8), kind=kLoop, calls=%fused_computation.2 | loop fusion | flops 24576 | bytes 196608 | tf_op jit(solution)/shard_map/convert_element_type | solution.py:369
  0.9 2.8 %copy-done = bf16[1,24,128,1024]{3,2,1,0:T(8,128)(2,1)S(1)} copy-done((bf16[1,24,128,1024]{3,2,1,0:T(8,128)(2,1)S(1)}, bf16[1,24,128,1024]{3,2,1,0:T(8,128)(2,1)}, u32[]{:S(2)}) %copy-start) | copy-done | bytes 6291480
  3.7 1.0 %shard_map.75 = (bf16[18,64,1024]{2,1,0:T(8,128)(2,1)S(1)}, bf16[18,64,1024]{2,1,0:T(8,128)(2,1)S(1)}) custom-call(s32[3]{0:T(128)S(1)} %compare_select_fusion.1.role, bf16[24,128,1024]{2,1,0:T(8,128)(2,1)S(1)} %bitcast.8, f32[24,1024]{1,0:T(8,128)S(1)} %convert_bitcast_fusion.mask), custom_call_target="tpu_custom_call" | custom-call | flops 2359296 | bytes 9437184 | tf_op jit(solution)/shard_map/pallas_call | solution.py:74
  4.9 0.7 shard_map.73
  6.2 4.3 %collective-permute-done.given = bf16[6,64,1024]{2,1,0:T(8,128)(2,1)S(1)} collective-permute-done((bf16[6,64,1024]{2,1,0:T(8,128)(2,1)S(1)}, bf16[6,64,1024]{2,1,0:T(8,128)(2,1)S(1)}, u32[]{:S(2)}, u32[]{:S(2)}) %collective-permute-start) | collective-permute-done | bytes 786464 | tf_op jit(solution)/shard_map/ppermute | solution.py:355
  10.5 2.2 %shard_map.74.own = bf16[2,6,64,512]{3,2,1,0:T(8,128)(2,1)S(1)} custom-call(s32[3]{0:T(128)S(1)} %compare_select_fusion.1.role, bf16[6,64,1024]{2,1,0:T(8,128)(2,1)S(1)} %get-tuple-element.22.kept, bf16[6,64,1024]{2,1,0:T(8,128)(2,1)S(1)} %collective-permute-done.given, bf16[1024,512]{1,0:T(8,128)(2,1)S(1)} %copy-done.1, bf16[512,256]{1,0:T(8,128)(2,1)S(1)} %copy-done.2), custom_call_target="tpu_custom_call" | custom-call | flops 1006632960 | bytes 2359296 | tf_op jit(solution)/shard_map/pallas_call | solution.py:124
  12.7 1.8 %collective-permute-start.8 = (bf16[2,6,64,512]{3,2,1,0:T(8,128)(2,1)S(1)}, bf16[2,6,64,512]{3,2,1,0:T(8,128)(2,1)S(1)}, u32[]{:S(2)}, u32[]{:S(2)}) collective-permute-start(bf16[2,6,64,512]{3,2,1,0:T(8,128)(2,1)S(1)} %shard_map.74.own), channel_id=1, source_target_pairs={{0,8},{1,9},{2,10},{3,11},{4,12},{5,13},{6,14},{7,15},{8,40},{9,41... | collective-permute-start | bytes 2359304 | tf_op jit(solution)/shard_map/ppermute | solution.py:355
  14.5 3.0 %shard_map.76.own = bf16[2,9,64,512]{3,2,1,0:T(8,128)(2,1)S(1)} custom-call(s32[3]{0:T(128)S(1)} %compare_select_fusion.1.role, bf16[18,64,1024]{2,1,0:T(8,128)(2,1)S(1)} %get-tuple-element.25.kept, bf16[18,64,1024]{2,1,0:T(8,128)(2,1)S(1)} %collective-permute-done.1.given, bf16[1024,512]{1,0:T(8,128)(2,1)S(1)} %copy-done.1, bf16[512,256]{1,0:T(8,128)(2,1)S(1)} %copy-done.2), custom_call_target="tpu_custom_call" | custom-call | flops 1509949440 | bytes 3538944 | tf_op jit(solution)/shard_map/pallas_call | solution.py:124
  17.7 1.5 %collective-permute-start.7 = (bf16[2,9,64,512]{3,2,1,0:T(8,128)(2,1)S(1)}, bf16[2,9,64,512]{3,2,1,0:T(8,128)(2,1)S(1)}, u32[]{:S(2)}, u32[]{:S(2)}) collective-permute-start(bf16[2,9,64,512]{3,2,1,0:T(8,128)(2,1)S(1)} %shard_map.76.own), channel_id=1, source_target_pairs={{0,8},{1,9},{2,10},{3,11},{4,12},{5,13},{6,14},{7,15},{8,24},{9,25... | collective-permute-start | bytes 3538952 | tf_op jit(solution)/shard_map/ppermute | solution.py:355
  19.2 2.9 %collective-permute-start.9 = (bf16[2,6,64,512]{3,2,1,0:T(8,128)(2,1)S(1)}, bf16[2,6,64,512]{3,2,1,0:T(8,128)(2,1)S(1)}, u32[]{:S(2)}, u32[]{:S(2)}) collective-permute-start(bf16[2,6,64,512]{3,2,1,0:T(8,128)(2,1)S(1)} %shard_map.74.own), channel_id=1, source_target_pairs={{0,8},{1,9},{2,10},{3,11},{4,12},{5,13},{6,14},{7,15},{8,24},{9,25... | collective-permute-start | bytes 2359304 | tf_op jit(solution)/shard_map/ppermute | solution.py:355
  22.1 2.2 %shard_map.77.own = bf16[2,6,64,512]{3,2,1,0:T(8,128)(2,1)S(1)} custom-call(s32[3]{0:T(128)S(1)} %compare_select_fusion.1.role, bf16[18,64,1024]{2,1,0:T(8,128)(2,1)S(1)} %get-tuple-element.25.kept, bf16[18,64,1024]{2,1,0:T(8,128)(2,1)S(1)} %collective-permute-done.1.given, bf16[1024,512]{1,0:T(8,128)(2,1)S(1)} %copy-done.1, bf16[512,256]{1,0:T(8,128)(2,1)S(1)} %copy-done.2), custom_call_target="tpu_custom_call" | custom-call | flops 1006632960 | bytes 2359296 | tf_op jit(solution)/shard_map/pallas_call | solution.py:124
  24.7 2.5 %collective-permute-start.5 = (bf16[2,6,64,512]{3,2,1,0:T(8,128)(2,1)S(1)}, bf16[2,6,64,512]{3,2,1,0:T(8,128)(2,1)S(1)}, u32[]{:S(2)}, u32[]{:S(2)}) collective-permute-start(bf16[2,6,64,512]{3,2,1,0:T(8,128)(2,1)S(1)} %shard_map.77.own), channel_id=1, source_target_pairs={{0,8},{1,9},{2,10},{3,11},{4,12},{5,13},{6,14},{7,15},{8,24},{9,25... | collective-permute-start | bytes 2359304 | tf_op jit(solution)/shard_map/ppermute | solution.py:355
  27.2 1.3 %shard_map.78.own = bf16[2,3,64,512]{3,2,1,0:T(8,128)(2,1)S(1)} custom-call(s32[3]{0:T(128)S(1)} %compare_select_fusion.1.role, bf16[18,64,1024]{2,1,0:T(8,128)(2,1)S(1)} %get-tuple-element.25.kept, bf16[18,64,1024]{2,1,0:T(8,128)(2,1)S(1)} %collective-permute-done.1.given, bf16[1024,512]{1,0:T(8,128)(2,1)S(1)} %copy-done.1, bf16[512,256]{1,0:T(8,128)(2,1)S(1)} %copy-done.2), custom_call_target="tpu_custom_call" | custom-call | flops 503316480 | bytes 1179648 | tf_op jit(solution)/shard_map/pallas_call | solution.py:124
  28.5 15.3 %collective-permute-done.9.across = bf16[2,6,64,512]{3,2,1,0:T(8,128)(2,1)S(1)} collective-permute-done((bf16[2,6,64,512]{3,2,1,0:T(8,128)(2,1)S(1)}, bf16[2,6,64,512]{3,2,1,0:T(8,128)(2,1)S(1)}, u32[]{:S(2)}, u32[]{:S(2)}) %collective-permute-start.9) | collective-permute-done | bytes 786464 | tf_op jit(solution)/shard_map/ppermute | solution.py:355
  43.9 2.6 %collective-permute-start.3 = (bf16[2,3,64,512]{3,2,1,0:T(8,128)(2,1)S(1)}, bf16[2,3,64,512]{3,2,1,0:T(8,128)(2,1)S(1)}, u32[]{:S(2)}, u32[]{:S(2)}) collective-permute-start(bf16[2,3,64,512]{3,2,1,0:T(8,128)(2,1)S(1)} %shard_map.78.own), channel_id=1, source_target_pairs={{0,8},{1,9},{2,10},{3,11},{4,12},{5,13},{6,14},{7,15},{8,24},{9,25... | collective-permute-start | bytes 1179656 | tf_op jit(solution)/shard_map/ppermute | solution.py:355
  46.5 3.4 %shard_map.79.refs_0_ = f32[104,768]{1,0:T(8,128)S(1)} custom-call(s32[3]{0:T(128)S(1)} %compare_select_fusion.1.role, bf16[2,6,64,512]{3,2,1,0:T(8,128)(2,1)S(1)} %shard_map.74.own, bf16[2,6,64,512]{3,2,1,0:T(8,128)(2,1)S(1)} %collective-permute-done.8.near, bf16[2,6,64,512]{3,2,1,0:T(8,128)(2,1)S(1)} %collective-permute-done.9.across, ...), custom_call_target="tpu_custom_call" | custom-call | flops 9437184 | bytes 2359296 | tf_op jit(solution)/shard_map/pallas_call | solution.py:262
  49.9 4.3 %shard_map.80.refs_0_ = f32[104,768]{1,0:T(8,128)S(1)} custom-call(s32[3]{0:T(128)S(1)} %compare_select_fusion.1.role, bf16[2,9,64,512]{3,2,1,0:T(8,128)(2,1)S(1)} %shard_map.76.own, bf16[2,9,64,512]{3,2,1,0:T(8,128)(2,1)S(1)} %collective-permute-done.6.near, bf16[2,9,64,512]{3,2,1,0:T(8,128)(2,1)S(1)} %collective-permute-done.7.across, ...), custom_call_target="tpu_custom_call" | custom-call | flops 14155776 | bytes 3538944 | tf_op jit(solution)/shard_map/pallas_call | solution.py:262
  54.3 3.4 %shard_map.81.refs_0_ = f32[104,768]{1,0:T(8,128)S(1)} custom-call(s32[3]{0:T(128)S(1)} %compare_select_fusion.1.role, bf16[2,6,64,512]{3,2,1,0:T(8,128)(2,1)S(1)} %shard_map.77.own, bf16[2,6,64,512]{3,2,1,0:T(8,128)(2,1)S(1)} %collective-permute-done.4.near, bf16[2,6,64,512]{3,2,1,0:T(8,128)(2,1)S(1)} %collective-permute-done.5.across, ...), custom_call_target="tpu_custom_call" | custom-call | flops 9437184 | bytes 2359296 | tf_op jit(solution)/shard_map/pallas_call | solution.py:262
  57.7 1.8 %shard_map.82 = (f32[104,512]{1,0:T(8,128)S(1)}, bf16[104,512]{1,0:T(8,128)(2,1)S(1)}, bf16[104,256]{1,0:T(8,128)(2,1)S(1)}) custom-call(s32[3]{0:T(128)S(1)} %compare_select_fusion.1.role, bf16[2,3,64,512]{3,2,1,0:T(8,128)(2,1)S(1)} %shard_map.78.own, bf16[2,3,64,512]{3,2,1,0:T(8,128)(2,1)S(1)} %collective-permute-done.2.near, ...), custom_call_target="tpu_custom_call" | custom-call | flops 4718592 | bytes 1179648 | tf_op jit(solution)/shard_map/pallas_call | solution.py:262
  59.5 1.0 %collective-permute-start.10 = (bf16[104,512]{1,0:T(8,128)(2,1)S(1)}, bf16[104,512]{1,0:T(8,128)(2,1)S(1)}, u32[]{:S(2)}, u32[]{:S(2)}) collective-permute-start(bf16[104,512]{1,0:T(8,128)(2,1)S(1)} %get-tuple-element.35), channel_id=1, source_target_pairs={{0,32},{1,33},{2,34},{3,35},{4,36},{5,37},{6,38},{7,39},{8,0},{9,1... | collective-permute-start | bytes 319496 | tf_op jit(solution)/shard_map/ppermute | solution.py:355
  60.5 1.8 %collective-permute-done.11.from_y = bf16[104,256]{1,0:T(8,128)(2,1)S(1)} collective-permute-done((bf16[104,256]{1,0:T(8,128)(2,1)S(1)}, bf16[104,256]{1,0:T(8,128)(2,1)S(1)}, u32[]{:S(2)}, u32[]{:S(2)}) %collective-permute-start.11) | collective-permute-done | bytes 53280 | tf_op jit(solution)/shard_map/ppermute | solution.py:355
  62.3 1.9 %collective-permute-done.10.from_z = bf16[104,512]{1,0:T(8,128)(2,1)S(1)} collective-permute-done((bf16[104,512]{1,0:T(8,128)(2,1)S(1)}, bf16[104,512]{1,0:T(8,128)(2,1)S(1)}, u32[]{:S(2)}, u32[]{:S(2)}) %collective-permute-start.10) | collective-permute-done | bytes 106528 | tf_op jit(solution)/shard_map/ppermute | solution.py:355
  64.8 0.6 collective-permute-start.12
  65.5 0.9 %collective-permute-done.12.got = bf16[104,256]{1,0:T(8,128)(2,1)S(1)} collective-permute-done((bf16[104,256]{1,0:T(8,128)(2,1)S(1)}, bf16[104,256]{1,0:T(8,128)(2,1)S(1)}, u32[]{:S(2)}, u32[]{:S(2)}) %collective-permute-start.12) | collective-permute-done | bytes 53280 | tf_op jit(solution)/shard_map/ppermute | solution.py:355
  66.4 0.7 assemble.1
  67.0 0.8 collective-permute-start.13
  67.8 4.5 %collective-permute-done.13 = bf16[104,512]{1,0:T(8,128)(2,1)S(1)} collective-permute-done((bf16[104,512]{1,0:T(8,128)(2,1)S(1)}, bf16[104,512]{1,0:T(8,128)(2,1)S(1)}, u32[]{:S(2)}, u32[]{:S(2)}) %collective-permute-start.13) | collective-permute-done | bytes 106528 | tf_op jit(solution)/shard_map/ppermute | solution.py:355
  72.4 1.6 %collective-permute-start.14 = (bf16[104,512]{1,0:T(8,128)(2,1)S(1)}, bf16[104,512]{1,0:T(8,128)(2,1)S(1)}, u32[]{:S(2)}, u32[]{:S(2)}) collective-permute-start(bf16[104,512]{1,0:T(8,128)(2,1)S(1)} %add_convert_fusion), channel_id=1, source_target_pairs={{0,1},{1,0},{2,3},{3,2},{4,5},{5,4},{6,7},{7,6},{8,9},{9,8},{10,11... | collective-permute-start | bytes 319496 | tf_op jit(solution)/shard_map/ppermute | solution.py:355
  74.0 2.7 %collective-permute-start.15 = (bf16[104,512]{1,0:T(8,128)(2,1)S(1)}, bf16[104,512]{1,0:T(8,128)(2,1)S(1)}, u32[]{:S(2)}, u32[]{:S(2)}) collective-permute-start(bf16[104,512]{1,0:T(8,128)(2,1)S(1)} %add_convert_fusion), channel_id=1, source_target_pairs={{0,2},{1,3},{2,0},{3,1},{4,6},{5,7},{6,4},{7,5},{8,10},{9,11},{10,... | collective-permute-start | bytes 319496 | tf_op jit(solution)/shard_map/ppermute | solution.py:355
  77.7 3.8 %collective-permute-done.15 = bf16[104,512]{1,0:T(8,128)(2,1)S(1)} collective-permute-done((bf16[104,512]{1,0:T(8,128)(2,1)S(1)}, bf16[104,512]{1,0:T(8,128)(2,1)S(1)}, u32[]{:S(2)}, u32[]{:S(2)}) %collective-permute-start.15) | collective-permute-done | bytes 106528 | tf_op jit(solution)/shard_map/ppermute | solution.py:355
  81.4 1.6 %collective-permute-done.16 = bf16[104,512]{1,0:T(8,128)(2,1)S(1)} collective-permute-done((bf16[104,512]{1,0:T(8,128)(2,1)S(1)}, bf16[104,512]{1,0:T(8,128)(2,1)S(1)}, u32[]{:S(2)}, u32[]{:S(2)}) %collective-permute-start.16) | collective-permute-done | bytes 106528 | tf_op jit(solution)/shard_map/ppermute | solution.py:355
  83.1 0.7 reshape.6
  (32 shorter events, 3.1 us)
Async XLA Ops:
  0.9 2.8 %copy-start = (bf16[1,24,128,1024]{3,2,1,0:T(8,128)(2,1)S(1)}, bf16[1,24,128,1024]{3,2,1,0:T(8,128)(2,1)}, u32[]{:S(2)}) copy-start(bf16[1,24,128,1024]{3,2,1,0:T(8,128)(2,1)} %param.7) | copy-start | bytes 18874372
  4.7 5.8 %copy-start.1 = (bf16[1024,512]{1,0:T(8,128)(2,1)S(1)}, bf16[1024,512]{1,0:T(8,128)(2,1)}, u32[]{:S(2)}) copy-start(bf16[1024,512]{1,0:T(8,128)(2,1)} %constant.56.clone.forward) | copy-start | bytes 3145732
  4.7 5.8 %copy-start.2 = (bf16[512,256]{1,0:T(8,128)(2,1)S(1)}, bf16[512,256]{1,0:T(8,128)(2,1)}, u32[]{:S(2)}) copy-start(bf16[512,256]{1,0:T(8,128)(2,1)} %constant.57.clone.band) | copy-start | bytes 786436
  4.8 9.8 %collective-permute-start.1 = (bf16[18,64,1024]{2,1,0:T(8,128)(2,1)S(1)}, bf16[18,64,1024]{2,1,0:T(8,128)(2,1)S(1)}, u32[]{:S(2)}, u32[]{:S(2)}) collective-permute-start(bf16[18,64,1024]{2,1,0:T(8,128)(2,1)S(1)} %get-tuple-element.26), channel_id=1, source_target_pairs={{0,8},{1,9},{2,10},{3,11},{4,12},{5,13},{6,14},{7,15},{8,0},{9,1},... | collective-permute-start | bytes 7077896 | tf_op jit(solution)/shard_map/ppermute | solution.py:355
  5.6 4.9 %collective-permute-start = (bf16[6,64,1024]{2,1,0:T(8,128)(2,1)S(1)}, bf16[6,64,1024]{2,1,0:T(8,128)(2,1)S(1)}, u32[]{:S(2)}, u32[]{:S(2)}) collective-permute-start(bf16[6,64,1024]{2,1,0:T(8,128)(2,1)S(1)} %get-tuple-element.23), channel_id=1, source_target_pairs={{0,8},{1,9},{2,10},{3,11},{4,12},{5,13},{6,14},{7,15},{8,0},{9,1},... | collective-permute-start | bytes 2359304 | tf_op jit(solution)/shard_map/ppermute | solution.py:355
  12.7 12.0 %collective-permute-start.8 = (bf16[2,6,64,512]{3,2,1,0:T(8,128)(2,1)S(1)}, bf16[2,6,64,512]{3,2,1,0:T(8,128)(2,1)S(1)}, u32[]{:S(2)}, u32[]{:S(2)}) collective-permute-start(bf16[2,6,64,512]{3,2,1,0:T(8,128)(2,1)S(1)} %shard_map.74.own), channel_id=1, source_target_pairs={{0,8},{1,9},{2,10},{3,11},{4,12},{5,13},{6,14},{7,15},{8,40},{9,41... | collective-permute-start | bytes 2359304 | tf_op jit(solution)/shard_map/ppermute | solution.py:355
  17.6 26.4 %collective-permute-start.6 = (bf16[2,9,64,512]{3,2,1,0:T(8,128)(2,1)S(1)}, bf16[2,9,64,512]{3,2,1,0:T(8,128)(2,1)S(1)}, u32[]{:S(2)}, u32[]{:S(2)}) collective-permute-start(bf16[2,9,64,512]{3,2,1,0:T(8,128)(2,1)S(1)} %shard_map.76.own), channel_id=1, source_target_pairs={{0,8},{1,9},{2,10},{3,11},{4,12},{5,13},{6,14},{7,15},{8,40},{9,41... | collective-permute-start | bytes 3538952 | tf_op jit(solution)/shard_map/ppermute | solution.py:355
  17.7 32.2 %collective-permute-start.7 = (bf16[2,9,64,512]{3,2,1,0:T(8,128)(2,1)S(1)}, bf16[2,9,64,512]{3,2,1,0:T(8,128)(2,1)S(1)}, u32[]{:S(2)}, u32[]{:S(2)}) collective-permute-start(bf16[2,9,64,512]{3,2,1,0:T(8,128)(2,1)S(1)} %shard_map.76.own), channel_id=1, source_target_pairs={{0,8},{1,9},{2,10},{3,11},{4,12},{5,13},{6,14},{7,15},{8,24},{9,25... | collective-permute-start | bytes 3538952 | tf_op jit(solution)/shard_map/ppermute | solution.py:355
  19.2 24.7 %collective-permute-start.9 = (bf16[2,6,64,512]{3,2,1,0:T(8,128)(2,1)S(1)}, bf16[2,6,64,512]{3,2,1,0:T(8,128)(2,1)S(1)}, u32[]{:S(2)}, u32[]{:S(2)}) collective-permute-start(bf16[2,6,64,512]{3,2,1,0:T(8,128)(2,1)S(1)} %shard_map.74.own), channel_id=1, source_target_pairs={{0,8},{1,9},{2,10},{3,11},{4,12},{5,13},{6,14},{7,15},{8,24},{9,25... | collective-permute-start | bytes 2359304 | tf_op jit(solution)/shard_map/ppermute | solution.py:355
  24.3 22.2 %copy-start.3 = (bf16[112,512]{1,0:T(8,128)(2,1)S(1)}, bf16[112,512]{1,0:T(8,128)(2,1)}, u32[]{:S(2)}) copy-start(bf16[112,512]{1,0:T(8,128)(2,1)} %constant.58.clone.refs_0_.refs_1_) | copy-start | bytes 344068
  24.3 22.2 %copy-start.4 = (bf16[112,512]{1,0:T(8,128)(2,1)S(1)}, bf16[112,512]{1,0:T(8,128)(2,1)}, u32[]{:S(2)}) copy-start(bf16[112,512]{1,0:T(8,128)(2,1)} %constant.59.clone.refs_1_.refs_2_) | copy-start | bytes 344068
  24.3 29.9 %collective-permute-start.4 = (bf16[2,6,64,512]{3,2,1,0:T(8,128)(2,1)S(1)}, bf16[2,6,64,512]{3,2,1,0:T(8,128)(2,1)S(1)}, u32[]{:S(2)}, u32[]{:S(2)}) collective-permute-start(bf16[2,6,64,512]{3,2,1,0:T(8,128)(2,1)S(1)} %shard_map.77.own), channel_id=1, source_target_pairs={{0,8},{1,9},{2,10},{3,11},{4,12},{5,13},{6,14},{7,15},{8,40},{9,41... | collective-permute-start | bytes 2359304 | tf_op jit(solution)/shard_map/ppermute | solution.py:355
  24.7 29.5 %collective-permute-start.5 = (bf16[2,6,64,512]{3,2,1,0:T(8,128)(2,1)S(1)}, bf16[2,6,64,512]{3,2,1,0:T(8,128)(2,1)S(1)}, u32[]{:S(2)}, u32[]{:S(2)}) collective-permute-start(bf16[2,6,64,512]{3,2,1,0:T(8,128)(2,1)S(1)} %shard_map.77.own), channel_id=1, source_target_pairs={{0,8},{1,9},{2,10},{3,11},{4,12},{5,13},{6,14},{7,15},{8,24},{9,25... | collective-permute-start | bytes 2359304 | tf_op jit(solution)/shard_map/ppermute | solution.py:355
  43.8 13.8 %collective-permute-start.2 = (bf16[2,3,64,512]{3,2,1,0:T(8,128)(2,1)S(1)}, bf16[2,3,64,512]{3,2,1,0:T(8,128)(2,1)S(1)}, u32[]{:S(2)}, u32[]{:S(2)}) collective-permute-start(bf16[2,3,64,512]{3,2,1,0:T(8,128)(2,1)S(1)} %shard_map.78.own), channel_id=1, source_target_pairs={{0,8},{1,9},{2,10},{3,11},{4,12},{5,13},{6,14},{7,15},{8,40},{9,41... | collective-permute-start | bytes 1179656 | tf_op jit(solution)/shard_map/ppermute | solution.py:355
  43.9 13.7 %collective-permute-start.3 = (bf16[2,3,64,512]{3,2,1,0:T(8,128)(2,1)S(1)}, bf16[2,3,64,512]{3,2,1,0:T(8,128)(2,1)S(1)}, u32[]{:S(2)}, u32[]{:S(2)}) collective-permute-start(bf16[2,3,64,512]{3,2,1,0:T(8,128)(2,1)S(1)} %shard_map.78.own), channel_id=1, source_target_pairs={{0,8},{1,9},{2,10},{3,11},{4,12},{5,13},{6,14},{7,15},{8,24},{9,25... | collective-permute-start | bytes 1179656 | tf_op jit(solution)/shard_map/ppermute | solution.py:355
  54.2 11.3 %copy-start.5 = (s32[1,4]{1,0:T(1,128)S(1)}, s32[1,4]{1,0:T(1,128)}, u32[]{:S(2)}) copy-start(s32[1,4]{1,0:T(1,128)} %param.9) | copy-start | bytes 52
  59.5 4.7 %collective-permute-start.10 = (bf16[104,512]{1,0:T(8,128)(2,1)S(1)}, bf16[104,512]{1,0:T(8,128)(2,1)S(1)}, u32[]{:S(2)}, u32[]{:S(2)}) collective-permute-start(bf16[104,512]{1,0:T(8,128)(2,1)S(1)} %get-tuple-element.35), channel_id=1, source_target_pairs={{0,32},{1,33},{2,34},{3,35},{4,36},{5,37},{6,38},{7,39},{8,0},{9,1... | collective-permute-start | bytes 319496 | tf_op jit(solution)/shard_map/ppermute | solution.py:355
  60.5 1.8 %collective-permute-start.11 = (bf16[104,256]{1,0:T(8,128)(2,1)S(1)}, bf16[104,256]{1,0:T(8,128)(2,1)S(1)}, u32[]{:S(2)}, u32[]{:S(2)}) collective-permute-start(bf16[104,256]{1,0:T(8,128)(2,1)S(1)} %get-tuple-element.36), channel_id=1, source_target_pairs={{0,16},{1,17},{2,18},{3,19},{4,20},{5,21},{6,22},{7,23},{8,0},{9,1... | collective-permute-start | bytes 159752 | tf_op jit(solution)/shard_map/ppermute | solution.py:355
  64.8 1.5 %collective-permute-start.12 = (bf16[104,256]{1,0:T(8,128)(2,1)S(1)}, bf16[104,256]{1,0:T(8,128)(2,1)S(1)}, u32[]{:S(2)}, u32[]{:S(2)}) collective-permute-start(bf16[104,256]{1,0:T(8,128)(2,1)S(1)} %get-tuple-element.38), channel_id=1, source_target_pairs={{0,8},{1,9},{2,10},{3,11},{4,12},{5,13},{6,14},{7,15},{8,0},{9,1},... | collective-permute-start | bytes 159752 | tf_op jit(solution)/shard_map/ppermute | solution.py:355
  67.0 5.3 %collective-permute-start.13 = (bf16[104,512]{1,0:T(8,128)(2,1)S(1)}, bf16[104,512]{1,0:T(8,128)(2,1)S(1)}, u32[]{:S(2)}, u32[]{:S(2)}) collective-permute-start(bf16[104,512]{1,0:T(8,128)(2,1)S(1)} %assemble.1), channel_id=1, source_target_pairs={{0,4},{1,5},{2,6},{3,7},{4,0},{5,1},{6,2},{7,3},{8,12},{9,13},{10,... | collective-permute-start | bytes 319496 | tf_op jit(solution)/shard_map/ppermute | solution.py:355
  72.4 5.3 %collective-permute-start.14 = (bf16[104,512]{1,0:T(8,128)(2,1)S(1)}, bf16[104,512]{1,0:T(8,128)(2,1)S(1)}, u32[]{:S(2)}, u32[]{:S(2)}) collective-permute-start(bf16[104,512]{1,0:T(8,128)(2,1)S(1)} %add_convert_fusion), channel_id=1, source_target_pairs={{0,1},{1,0},{2,3},{3,2},{4,5},{5,4},{6,7},{7,6},{8,9},{9,8},{10,11... | collective-permute-start | bytes 319496 | tf_op jit(solution)/shard_map/ppermute | solution.py:355
  74.0 7.5 %collective-permute-start.15 = (bf16[104,512]{1,0:T(8,128)(2,1)S(1)}, bf16[104,512]{1,0:T(8,128)(2,1)S(1)}, u32[]{:S(2)}, u32[]{:S(2)}) collective-permute-start(bf16[104,512]{1,0:T(8,128)(2,1)S(1)} %add_convert_fusion), channel_id=1, source_target_pairs={{0,2},{1,3},{2,0},{3,1},{4,6},{5,7},{6,4},{7,5},{8,10},{9,11},{10,... | collective-permute-start | bytes 319496 | tf_op jit(solution)/shard_map/ppermute | solution.py:355
  76.7 6.4 %collective-permute-start.16 = (bf16[104,512]{1,0:T(8,128)(2,1)S(1)}, bf16[104,512]{1,0:T(8,128)(2,1)S(1)}, u32[]{:S(2)}, u32[]{:S(2)}) collective-permute-start(bf16[104,512]{1,0:T(8,128)(2,1)S(1)} %add_convert_fusion), channel_id=1, source_target_pairs={{0,3},{1,2},{2,1},{3,0},{4,7},{5,6},{6,5},{7,4},{8,11},{9,10},{10,... | collective-permute-start | bytes 319496 | tf_op jit(solution)/shard_map/ppermute | solution.py:355

commit v2 on v1

--- a/solution.py
+++ b/solution.py
@@ -21,7 +21,7 @@
 STEP = 3
 TILE = 16
 PLANES = 12
-CHUNKS = ((0, 6), (6, 9), (15, 6), (21, 3))
+CHUNKS = ((0, 6), (6, 12), (18, 3), (21, 3))
 VMEM = 24 << 20
 WATER = 0.05
 EPS = 1e-06
@@ -62,7 +62,7 @@
     i = pl.program_id(0)
     core = role[1]
     for j in range(STEP):
-        keep = mask[pl.ds(first + i * STEP + j, 1), :].astype(bf16)
+        keep = mask[pl.ds(first + i * STEP + j, 1), :].astype(f32).astype(bf16)
         own[j] = traces[j, pl.ds(pl.multiple_of(core * HALF, HALF), HALF), :] * keep
         give[j] = traces[j, pl.ds(pl.multiple_of((1 - core) * HALF, HALF), HALF), :] * keep
 
@@ -366,7 +366,7 @@
     forward, band = jnp.asarray(forward_table()), jnp.asarray(band_table())
     high, low = inverse_tables(windows_all)
     tables = (jnp.asarray(high), jnp.asarray(low))
-    mask = valid_mask[0].astype(f32)
+    mask = valid_mask[0]
 
     rest = CHUNKS[0][1]
     later = traces.shape[1] - rest

time: 84 us -> 89.3 us (1.063)
  the two profiles are of different devices: /device:TPU:32 before, /device:TPU:96 now
where the time goes in v2:
time: 89.3 us; the launch traced here: 89.2 us
  waiting for transfers between devices  40.9 us (46%)
  Pallas kernels  24.3 us (27%)
  starting transfers between devices  19.1 us (21%)
  local copies, waits for them, and re-layouts  4.46 us (5%)
    ppermute x17, waiting for transfers between devices, move(): return lax.ppermute(block, ('chan', 'tm'), route(blocks, times, target))  40.9 us
    ppermute x17, starting transfers between devices, move(): return lax.ppermute(block, ('chan', 'tm'), route(blocks, times, target))  19.1 us
    pallas_call x4, Pallas kernels, cross(): pl.pallas_call(functools.partial(cross_kernel, start, last), in_specs=[pl...  12.7 us
    pallas_call x4, Pallas kernels, whiten(): pl.pallas_call(whiten_kernel, grid_spec=pltpu.PrefetchScalarGridSpec(num_...  8.64 us
    unnamed x14, local copies, waits for them, and re-layouts  3.71 us
  transfers between devices with their start and end apart: 17, of which 9 were waited for; matrix products, arithmetic and copies ran while one was open for 0% of the time, Pallas kernels for 18%

profile of v2, /device:TPU:96, one launch (start us, length us, event | category | flops | bytes accessed | tf_op | source)
XLA Modules:
  0.0 89.2 jit_solution(2947902385802975016)
XLA Ops:
  0.0 2.8 %copy-done = bf16[1,24,128,1024]{3,2,1,0:T(8,128)(2,1)S(1)} copy-done((bf16[1,24,128,1024]{3,2,1,0:T(8,128)(2,1)S(1)}, bf16[1,24,128,1024]{3,2,1,0:T(8,128)(2,1)}, u32[]{:S(2)}) %copy-start) | copy-done | bytes 6291480
  2.8 0.9 copy-done.5
  3.7 1.0 %shard_map.75 = (bf16[18,64,1024]{2,1,0:T(8,128)(2,1)S(1)}, bf16[18,64,1024]{2,1,0:T(8,128)(2,1)S(1)}) custom-call(s32[3]{0:T(128)S(1)} %compare_select_fusion.1.role, bf16[24,128,1024]{2,1,0:T(8,128)(2,1)S(1)} %bitcast.7, s32[24,1024]{1,0:T(8,128)S(1)} %bitcast.9), custom_call_target="tpu_custom_call" | custom-call | flops 2359296 | bytes 9437184 | tf_op jit(solution)/shard_map/pallas_call | solution.py:74
  4.8 0.7 shard_map.73
  5.6 0.6 collective-permute-start
  6.2 4.3 %collective-permute-done.given = bf16[6,64,1024]{2,1,0:T(8,128)(2,1)S(1)} collective-permute-done((bf16[6,64,1024]{2,1,0:T(8,128)(2,1)S(1)}, bf16[6,64,1024]{2,1,0:T(8,128)(2,1)S(1)}, u32[]{:S(2)}, u32[]{:S(2)}) %collective-permute-start) | collective-permute-done | bytes 786464 | tf_op jit(solution)/shard_map/ppermute | solution.py:355
  10.5 2.2 %shard_map.74.own = bf16[2,6,64,512]{3,2,1,0:T(8,128)(2,1)S(1)} custom-call(s32[3]{0:T(128)S(1)} %compare_select_fusion.1.role, bf16[6,64,1024]{2,1,0:T(8,128)(2,1)S(1)} %get-tuple-element.22.kept, bf16[6,64,1024]{2,1,0:T(8,128)(2,1)S(1)} %collective-permute-done.given, bf16[1024,512]{1,0:T(8,128)(2,1)S(1)} %copy-done.1, bf16[512,256]{1,0:T(8,128)(2,1)S(1)} %copy-done.2), custom_call_target="tpu_custom_call" | custom-call | flops 1006632960 | bytes 2359296 | tf_op jit(solution)/shard_map/pallas_call | solution.py:124
  12.7 3.8 %shard_map.76.own = bf16[2,12,64,512]{3,2,1,0:T(8,128)(2,1)S(1)} custom-call(s32[3]{0:T(128)S(1)} %compare_select_fusion.1.role, bf16[18,64,1024]{2,1,0:T(8,128)(2,1)S(1)} %get-tuple-element.25.kept, bf16[18,64,1024]{2,1,0:T(8,128)(2,1)S(1)} %collective-permute-done.1.given, bf16[1024,512]{1,0:T(8,128)(2,1)S(1)} %copy-done.1, bf16[512,256]{1,0:T(8,128)(2,1)S(1)} %copy-done.2), custom_call_target="tpu_custom_call" | custom-call | flops 2013265920 | bytes 4718592 | tf_op jit(solution)/shard_map/pallas_call | solution.py:124
  16.7 2.9 %collective-permute-start.7 = (bf16[2,12,64,512]{3,2,1,0:T(8,128)(2,1)S(1)}, bf16[2,12,64,512]{3,2,1,0:T(8,128)(2,1)S(1)}, u32[]{:S(2)}, u32[]{:S(2)}) collective-permute-start(bf16[2,12,64,512]{3,2,1,0:T(8,128)(2,1)S(1)} %shard_map.76.own), channel_id=1, source_target_pairs={{0,8},{1,9},{2,10},{3,11},{4,12},{5,13},{6,14},{7,15},{8,24},{9,25... | collective-permute-start | bytes 4718600 | tf_op jit(solution)/shard_map/ppermute | solution.py:355
  19.5 3.6 %collective-permute-start.9 = (bf16[2,6,64,512]{3,2,1,0:T(8,128)(2,1)S(1)}, bf16[2,6,64,512]{3,2,1,0:T(8,128)(2,1)S(1)}, u32[]{:S(2)}, u32[]{:S(2)}) collective-permute-start(bf16[2,6,64,512]{3,2,1,0:T(8,128)(2,1)S(1)} %shard_map.74.own), channel_id=1, source_target_pairs={{0,8},{1,9},{2,10},{3,11},{4,12},{5,13},{6,14},{7,15},{8,24},{9,25... | collective-permute-start | bytes 2359304 | tf_op jit(solution)/shard_map/ppermute | solution.py:355
  23.2 1.3 %shard_map.77.own = bf16[2,3,64,512]{3,2,1,0:T(8,128)(2,1)S(1)} custom-call(s32[3]{0:T(128)S(1)} %compare_select_fusion.1.role, bf16[18,64,1024]{2,1,0:T(8,128)(2,1)S(1)} %get-tuple-element.25.kept, bf16[18,64,1024]{2,1,0:T(8,128)(2,1)S(1)} %collective-permute-done.1.given, bf16[1024,512]{1,0:T(8,128)(2,1)S(1)} %copy-done.1, bf16[512,256]{1,0:T(8,128)(2,1)S(1)} %copy-done.2), custom_call_target="tpu_custom_call" | custom-call | flops 503316480 | bytes 1179648 | tf_op jit(solution)/shard_map/pallas_call | solution.py:124
  24.5 1.0 %collective-permute-start.4 = (bf16[2,3,64,512]{3,2,1,0:T(8,128)(2,1)S(1)}, bf16[2,3,64,512]{3,2,1,0:T(8,128)(2,1)S(1)}, u32[]{:S(2)}, u32[]{:S(2)}) collective-permute-start(bf16[2,3,64,512]{3,2,1,0:T(8,128)(2,1)S(1)} %shard_map.77.own), channel_id=1, source_target_pairs={{0,8},{1,9},{2,10},{3,11},{4,12},{5,13},{6,14},{7,15},{8,40},{9,41... | collective-permute-start | bytes 1179656 | tf_op jit(solution)/shard_map/ppermute | solution.py:355
  25.6 21.1 %collective-permute-done.8.near = bf16[2,6,64,512]{3,2,1,0:T(8,128)(2,1)S(1)} collective-permute-done((bf16[2,6,64,512]{3,2,1,0:T(8,128)(2,1)S(1)}, bf16[2,6,64,512]{3,2,1,0:T(8,128)(2,1)S(1)}, u32[]{:S(2)}, u32[]{:S(2)}) %collective-permute-start.8) | collective-permute-done | bytes 786464 | tf_op jit(solution)/shard_map/ppermute | solution.py:355
  46.6 1.3 %shard_map.78.own = bf16[2,3,64,512]{3,2,1,0:T(8,128)(2,1)S(1)} custom-call(s32[3]{0:T(128)S(1)} %compare_select_fusion.1.role, bf16[18,64,1024]{2,1,0:T(8,128)(2,1)S(1)} %get-tuple-element.25.kept, bf16[18,64,1024]{2,1,0:T(8,128)(2,1)S(1)} %collective-permute-done.1.given, bf16[1024,512]{1,0:T(8,128)(2,1)S(1)} %copy-done.1, bf16[512,256]{1,0:T(8,128)(2,1)S(1)} %copy-done.2), custom_call_target="tpu_custom_call" | custom-call | flops 503316480 | bytes 1179648 | tf_op jit(solution)/shard_map/pallas_call | solution.py:124
  48.0 4.7 %collective-permute-start.3 = (bf16[2,3,64,512]{3,2,1,0:T(8,128)(2,1)S(1)}, bf16[2,3,64,512]{3,2,1,0:T(8,128)(2,1)S(1)}, u32[]{:S(2)}, u32[]{:S(2)}) collective-permute-start(bf16[2,3,64,512]{3,2,1,0:T(8,128)(2,1)S(1)} %shard_map.78.own), channel_id=1, source_target_pairs={{0,8},{1,9},{2,10},{3,11},{4,12},{5,13},{6,14},{7,15},{8,24},{9,25... | collective-permute-start | bytes 1179656 | tf_op jit(solution)/shard_map/ppermute | solution.py:355
  52.7 3.4 %shard_map.79.refs_0_ = f32[104,768]{1,0:T(8,128)S(1)} custom-call(s32[3]{0:T(128)S(1)} %compare_select_fusion.1.role, bf16[2,6,64,512]{3,2,1,0:T(8,128)(2,1)S(1)} %shard_map.74.own, bf16[2,6,64,512]{3,2,1,0:T(8,128)(2,1)S(1)} %collective-permute-done.8.near, bf16[2,6,64,512]{3,2,1,0:T(8,128)(2,1)S(1)} %collective-permute-done.9.across, ...), custom_call_target="tpu_custom_call" | custom-call | flops 9437184 | bytes 2359296 | tf_op jit(solution)/shard_map/pallas_call | solution.py:262
  56.1 5.2 %shard_map.80.refs_0_ = f32[104,768]{1,0:T(8,128)S(1)} custom-call(s32[3]{0:T(128)S(1)} %compare_select_fusion.1.role, bf16[2,12,64,512]{3,2,1,0:T(8,128)(2,1)S(1)} %shard_map.76.own, bf16[2,12,64,512]{3,2,1,0:T(8,128)(2,1)S(1)} %collective-permute-done.6.near, bf16[2,12,64,512]{3,2,1,0:T(8,128)(2,1)S(1)} %collective-permute-done.7.across, ...), custom_call_target="tpu_custom_call" | custom-call | flops 18874368 | bytes 4718592 | tf_op jit(solution)/shard_map/pallas_call | solution.py:262
  61.3 2.3 %shard_map.81.refs_0_ = f32[104,768]{1,0:T(8,128)S(1)} custom-call(s32[3]{0:T(128)S(1)} %compare_select_fusion.1.role, bf16[2,3,64,512]{3,2,1,0:T(8,128)(2,1)S(1)} %shard_map.77.own, bf16[2,3,64,512]{3,2,1,0:T(8,128)(2,1)S(1)} %collective-permute-done.4.near, bf16[2,3,64,512]{3,2,1,0:T(8,128)(2,1)S(1)} %collective-permute-done.5.across, ...), custom_call_target="tpu_custom_call" | custom-call | flops 4718592 | bytes 1179648 | tf_op jit(solution)/shard_map/pallas_call | solution.py:262
  63.7 1.8 %shard_map.82 = (f32[104,512]{1,0:T(8,128)S(1)}, bf16[104,512]{1,0:T(8,128)(2,1)S(1)}, bf16[104,256]{1,0:T(8,128)(2,1)S(1)}) custom-call(s32[3]{0:T(128)S(1)} %compare_select_fusion.1.role, bf16[2,3,64,512]{3,2,1,0:T(8,128)(2,1)S(1)} %shard_map.78.own, bf16[2,3,64,512]{3,2,1,0:T(8,128)(2,1)S(1)} %collective-permute-done.2.near, ...), custom_call_target="tpu_custom_call" | custom-call | flops 4718592 | bytes 1179648 | tf_op jit(solution)/shard_map/pallas_call | solution.py:262
  65.9 1.8 %collective-permute-done.11.from_y = bf16[104,256]{1,0:T(8,128)(2,1)S(1)} collective-permute-done((bf16[104,256]{1,0:T(8,128)(2,1)S(1)}, bf16[104,256]{1,0:T(8,128)(2,1)S(1)}, u32[]{:S(2)}, u32[]{:S(2)}) %collective-permute-start.11) | collective-permute-done | bytes 53280 | tf_op jit(solution)/shard_map/ppermute | solution.py:355
  67.7 2.5 %collective-permute-done.10.from_z = bf16[104,512]{1,0:T(8,128)(2,1)S(1)} collective-permute-done((bf16[104,512]{1,0:T(8,128)(2,1)S(1)}, bf16[104,512]{1,0:T(8,128)(2,1)S(1)}, u32[]{:S(2)}, u32[]{:S(2)}) %collective-permute-start.10) | collective-permute-done | bytes 106528 | tf_op jit(solution)/shard_map/ppermute | solution.py:355
  70.2 0.6 combine.1
  70.9 1.2 %collective-permute-done.12.got = bf16[104,256]{1,0:T(8,128)(2,1)S(1)} collective-permute-done((bf16[104,256]{1,0:T(8,128)(2,1)S(1)}, bf16[104,256]{1,0:T(8,128)(2,1)S(1)}, u32[]{:S(2)}, u32[]{:S(2)}) %collective-permute-start.12) | collective-permute-done | bytes 53280 | tf_op jit(solution)/shard_map/ppermute | solution.py:355
  72.1 0.7 assemble.1
  72.8 0.8 collective-permute-start.13
  73.6 4.4 %collective-permute-done.13 = bf16[104,512]{1,0:T(8,128)(2,1)S(1)} collective-permute-done((bf16[104,512]{1,0:T(8,128)(2,1)S(1)}, bf16[104,512]{1,0:T(8,128)(2,1)S(1)}, u32[]{:S(2)}, u32[]{:S(2)}) %collective-permute-start.13) | collective-permute-done | bytes 106528 | tf_op jit(solution)/shard_map/ppermute | solution.py:355
  78.0 1.6 %collective-permute-start.14 = (bf16[104,512]{1,0:T(8,128)(2,1)S(1)}, bf16[104,512]{1,0:T(8,128)(2,1)S(1)}, u32[]{:S(2)}, u32[]{:S(2)}) collective-permute-start(bf16[104,512]{1,0:T(8,128)(2,1)S(1)} %add_convert_fusion), channel_id=1, source_target_pairs={{0,1},{1,0},{2,3},{3,2},{4,5},{5,4},{6,7},{7,6},{8,9},{9,8},{10,11... | collective-permute-start | bytes 319496 | tf_op jit(solution)/shard_map/ppermute | solution.py:355
  79.6 2.7 %collective-permute-start.15 = (bf16[104,512]{1,0:T(8,128)(2,1)S(1)}, bf16[104,512]{1,0:T(8,128)(2,1)S(1)}, u32[]{:S(2)}, u32[]{:S(2)}) collective-permute-start(bf16[104,512]{1,0:T(8,128)(2,1)S(1)} %add_convert_fusion), channel_id=1, source_target_pairs={{0,2},{1,3},{2,0},{3,1},{4,6},{5,7},{6,4},{7,5},{8,10},{9,11},{10,... | collective-permute-start | bytes 319496 | tf_op jit(solution)/shard_map/ppermute | solution.py:355
  82.8 0.7 collective-permute-done.14
  83.4 3.4 %collective-permute-done.15 = bf16[104,512]{1,0:T(8,128)(2,1)S(1)} collective-permute-done((bf16[104,512]{1,0:T(8,128)(2,1)S(1)}, bf16[104,512]{1,0:T(8,128)(2,1)S(1)}, u32[]{:S(2)}, u32[]{:S(2)}) %collective-permute-start.15) | collective-permute-done | bytes 106528 | tf_op jit(solution)/shard_map/ppermute | solution.py:355
  86.8 1.5 %collective-permute-done.16 = bf16[104,512]{1,0:T(8,128)(2,1)S(1)} collective-permute-done((bf16[104,512]{1,0:T(8,128)(2,1)S(1)}, bf16[104,512]{1,0:T(8,128)(2,1)S(1)}, u32[]{:S(2)}, u32[]{:S(2)}) %collective-permute-start.16) | collective-permute-done | bytes 106528 | tf_op jit(solution)/shard_map/ppermute | solution.py:355
  88.4 0.7 reshape.5
  (33 shorter events, 1.4 us)
Async XLA Ops:
  0.0 2.8 %copy-start = (bf16[1,24,128,1024]{3,2,1,0:T(8,128)(2,1)S(1)}, bf16[1,24,128,1024]{3,2,1,0:T(8,128)(2,1)}, u32[]{:S(2)}) copy-start(bf16[1,24,128,1024]{3,2,1,0:T(8,128)(2,1)} %param.7) | copy-start | bytes 18874372
  2.8 0.9 %copy-start.5 = (s32[1,24,1024]{2,1,0:T(8,128)S(1)}, s32[1,24,1024]{2,1,0:T(8,128)}, u32[]{:S(2)}) copy-start(s32[1,24,1024]{2,1,0:T(8,128)} %param.8) | copy-start | bytes 294916
  4.7 5.8 %copy-start.1 = (bf16[1024,512]{1,0:T(8,128)(2,1)S(1)}, bf16[1024,512]{1,0:T(8,128)(2,1)}, u32[]{:S(2)}) copy-start(bf16[1024,512]{1,0:T(8,128)(2,1)} %constant.56.clone.forward) | copy-start | bytes 3145732
  4.7 5.8 %copy-start.2 = (bf16[512,256]{1,0:T(8,128)(2,1)S(1)}, bf16[512,256]{1,0:T(8,128)(2,1)}, u32[]{:S(2)}) copy-start(bf16[512,256]{1,0:T(8,128)(2,1)} %constant.57.clone.band) | copy-start | bytes 786436
  4.7 8.0 %collective-permute-start.1 = (bf16[18,64,1024]{2,1,0:T(8,128)(2,1)S(1)}, bf16[18,64,1024]{2,1,0:T(8,128)(2,1)S(1)}, u32[]{:S(2)}, u32[]{:S(2)}) collective-permute-start(bf16[18,64,1024]{2,1,0:T(8,128)(2,1)S(1)} %get-tuple-element.26), channel_id=1, source_target_pairs={{0,8},{1,9},{2,10},{3,11},{4,12},{5,13},{6,14},{7,15},{8,0},{9,1},... | collective-permute-start | bytes 7077896 | tf_op jit(solution)/shard_map/ppermute | solution.py:355
  5.6 4.9 %collective-permute-start = (bf16[6,64,1024]{2,1,0:T(8,128)(2,1)S(1)}, bf16[6,64,1024]{2,1,0:T(8,128)(2,1)S(1)}, u32[]{:S(2)}, u32[]{:S(2)}) collective-permute-start(bf16[6,64,1024]{2,1,0:T(8,128)(2,1)S(1)} %get-tuple-element.23), channel_id=1, source_target_pairs={{0,8},{1,9},{2,10},{3,11},{4,12},{5,13},{6,14},{7,15},{8,0},{9,1},... | collective-permute-start | bytes 2359304 | tf_op jit(solution)/shard_map/ppermute | solution.py:355
  16.5 31.4 %collective-permute-start.6 = (bf16[2,12,64,512]{3,2,1,0:T(8,128)(2,1)S(1)}, bf16[2,12,64,512]{3,2,1,0:T(8,128)(2,1)S(1)}, u32[]{:S(2)}, u32[]{:S(2)}) collective-permute-start(bf16[2,12,64,512]{3,2,1,0:T(8,128)(2,1)S(1)} %shard_map.76.own), channel_id=1, source_target_pairs={{0,8},{1,9},{2,10},{3,11},{4,12},{5,13},{6,14},{7,15},{8,40},{9,41... | collective-permute-start | bytes 4718600 | tf_op jit(solution)/shard_map/ppermute | solution.py:355
  16.7 39.4 %collective-permute-start.7 = (bf16[2,12,64,512]{3,2,1,0:T(8,128)(2,1)S(1)}, bf16[2,12,64,512]{3,2,1,0:T(8,128)(2,1)S(1)}, u32[]{:S(2)}, u32[]{:S(2)}) collective-permute-start(bf16[2,12,64,512]{3,2,1,0:T(8,128)(2,1)S(1)} %shard_map.76.own), channel_id=1, source_target_pairs={{0,8},{1,9},{2,10},{3,11},{4,12},{5,13},{6,14},{7,15},{8,24},{9,25... | collective-permute-start | bytes 4718600 | tf_op jit(solution)/shard_map/ppermute | solution.py:355
  19.5 27.1 %collective-permute-start.8 = (bf16[2,6,64,512]{3,2,1,0:T(8,128)(2,1)S(1)}, bf16[2,6,64,512]{3,2,1,0:T(8,128)(2,1)S(1)}, u32[]{:S(2)}, u32[]{:S(2)}) collective-permute-start(bf16[2,6,64,512]{3,2,1,0:T(8,128)(2,1)S(1)} %shard_map.74.own), channel_id=1, source_target_pairs={{0,8},{1,9},{2,10},{3,11},{4,12},{5,13},{6,14},{7,15},{8,40},{9,41... | collective-permute-start | bytes 2359304 | tf_op jit(solution)/shard_map/ppermute | solution.py:355
  19.5 28.4 %collective-permute-start.9 = (bf16[2,6,64,512]{3,2,1,0:T(8,128)(2,1)S(1)}, bf16[2,6,64,512]{3,2,1,0:T(8,128)(2,1)S(1)}, u32[]{:S(2)}, u32[]{:S(2)}) collective-permute-start(bf16[2,6,64,512]{3,2,1,0:T(8,128)(2,1)S(1)} %shard_map.74.own), channel_id=1, source_target_pairs={{0,8},{1,9},{2,10},{3,11},{4,12},{5,13},{6,14},{7,15},{8,24},{9,25... | collective-permute-start | bytes 2359304 | tf_op jit(solution)/shard_map/ppermute | solution.py:355
  24.5 28.2 %copy-start.3 = (bf16[112,512]{1,0:T(8,128)(2,1)S(1)}, bf16[112,512]{1,0:T(8,128)(2,1)}, u32[]{:S(2)}) copy-start(bf16[112,512]{1,0:T(8,128)(2,1)} %constant.58.clone.refs_0_.refs_1_) | copy-start | bytes 344068
  24.5 28.2 %copy-start.4 = (bf16[112,512]{1,0:T(8,128)(2,1)S(1)}, bf16[112,512]{1,0:T(8,128)(2,1)}, u32[]{:S(2)}) copy-start(bf16[112,512]{1,0:T(8,128)(2,1)} %constant.59.clone.refs_1_.refs_2_) | copy-start | bytes 344068
  24.5 36.8 %collective-permute-start.4 = (bf16[2,3,64,512]{3,2,1,0:T(8,128)(2,1)S(1)}, bf16[2,3,64,512]{3,2,1,0:T(8,128)(2,1)S(1)}, u32[]{:S(2)}, u32[]{:S(2)}) collective-permute-start(bf16[2,3,64,512]{3,2,1,0:T(8,128)(2,1)S(1)} %shard_map.77.own), channel_id=1, source_target_pairs={{0,8},{1,9},{2,10},{3,11},{4,12},{5,13},{6,14},{7,15},{8,40},{9,41... | collective-permute-start | bytes 1179656 | tf_op jit(solution)/shard_map/ppermute | solution.py:355
  46.6 14.7 %collective-permute-start.5 = (bf16[2,3,64,512]{3,2,1,0:T(8,128)(2,1)S(1)}, bf16[2,3,64,512]{3,2,1,0:T(8,128)(2,1)S(1)}, u32[]{:S(2)}, u32[]{:S(2)}) collective-permute-start(bf16[2,3,64,512]{3,2,1,0:T(8,128)(2,1)S(1)} %shard_map.77.own), channel_id=1, source_target_pairs={{0,8},{1,9},{2,10},{3,11},{4,12},{5,13},{6,14},{7,15},{8,24},{9,25... | collective-permute-start | bytes 1179656 | tf_op jit(solution)/shard_map/ppermute | solution.py:355
  47.9 15.7 %collective-permute-start.2 = (bf16[2,3,64,512]{3,2,1,0:T(8,128)(2,1)S(1)}, bf16[2,3,64,512]{3,2,1,0:T(8,128)(2,1)S(1)}, u32[]{:S(2)}, u32[]{:S(2)}) collective-permute-start(bf16[2,3,64,512]{3,2,1,0:T(8,128)(2,1)S(1)} %shard_map.78.own), channel_id=1, source_target_pairs={{0,8},{1,9},{2,10},{3,11},{4,12},{5,13},{6,14},{7,15},{8,40},{9,41... | collective-permute-start | bytes 1179656 | tf_op jit(solution)/shard_map/ppermute | solution.py:355
  48.0 15.7 %collective-permute-start.3 = (bf16[2,3,64,512]{3,2,1,0:T(8,128)(2,1)S(1)}, bf16[2,3,64,512]{3,2,1,0:T(8,128)(2,1)S(1)}, u32[]{:S(2)}, u32[]{:S(2)}) collective-permute-start(bf16[2,3,64,512]{3,2,1,0:T(8,128)(2,1)S(1)} %shard_map.78.own), channel_id=1, source_target_pairs={{0,8},{1,9},{2,10},{3,11},{4,12},{5,13},{6,14},{7,15},{8,24},{9,25... | collective-permute-start | bytes 1179656 | tf_op jit(solution)/shard_map/ppermute | solution.py:355
  61.3 9.6 %copy-start.6 = (s32[1,4]{1,0:T(1,128)S(1)}, s32[1,4]{1,0:T(1,128)}, u32[]{:S(2)}) copy-start(s32[1,4]{1,0:T(1,128)} %param.9) | copy-start | bytes 52
  65.5 4.7 %collective-permute-start.10 = (bf16[104,512]{1,0:T(8,128)(2,1)S(1)}, bf16[104,512]{1,0:T(8,128)(2,1)S(1)}, u32[]{:S(2)}, u32[]{:S(2)}) collective-permute-start(bf16[104,512]{1,0:T(8,128)(2,1)S(1)} %get-tuple-element.35), channel_id=1, source_target_pairs={{0,32},{1,33},{2,34},{3,35},{4,36},{5,37},{6,38},{7,39},{8,0},{9,1... | collective-permute-start | bytes 319496 | tf_op jit(solution)/shard_map/ppermute | solution.py:355
  65.9 1.8 %collective-permute-start.11 = (bf16[104,256]{1,0:T(8,128)(2,1)S(1)}, bf16[104,256]{1,0:T(8,128)(2,1)S(1)}, u32[]{:S(2)}, u32[]{:S(2)}) collective-permute-start(bf16[104,256]{1,0:T(8,128)(2,1)S(1)} %get-tuple-element.36), channel_id=1, source_target_pairs={{0,16},{1,17},{2,18},{3,19},{4,20},{5,21},{6,22},{7,23},{8,0},{9,1... | collective-permute-start | bytes 159752 | tf_op jit(solution)/shard_map/ppermute | solution.py:355
  70.8 1.3 %collective-permute-start.12 = (bf16[104,256]{1,0:T(8,128)(2,1)S(1)}, bf16[104,256]{1,0:T(8,128)(2,1)S(1)}, u32[]{:S(2)}, u32[]{:S(2)}) collective-permute-start(bf16[104,256]{1,0:T(8,128)(2,1)S(1)} %get-tuple-element.38), channel_id=1, source_target_pairs={{0,8},{1,9},{2,10},{3,11},{4,12},{5,13},{6,14},{7,15},{8,0},{9,1},... | collective-permute-start | bytes 159752 | tf_op jit(solution)/shard_map/ppermute | solution.py:355
  72.8 5.1 %collective-permute-start.13 = (bf16[104,512]{1,0:T(8,128)(2,1)S(1)}, bf16[104,512]{1,0:T(8,128)(2,1)S(1)}, u32[]{:S(2)}, u32[]{:S(2)}) collective-permute-start(bf16[104,512]{1,0:T(8,128)(2,1)S(1)} %assemble.1), channel_id=1, source_target_pairs={{0,4},{1,5},{2,6},{3,7},{4,0},{5,1},{6,2},{7,3},{8,12},{9,13},{10,... | collective-permute-start | bytes 319496 | tf_op jit(solution)/shard_map/ppermute | solution.py:355
  78.0 5.4 %collective-permute-start.14 = (bf16[104,512]{1,0:T(8,128)(2,1)S(1)}, bf16[104,512]{1,0:T(8,128)(2,1)S(1)}, u32[]{:S(2)}, u32[]{:S(2)}) collective-permute-start(bf16[104,512]{1,0:T(8,128)(2,1)S(1)} %add_convert_fusion), channel_id=1, source_target_pairs={{0,1},{1,0},{2,3},{3,2},{4,5},{5,4},{6,7},{7,6},{8,9},{9,8},{10,11... | collective-permute-start | bytes 319496 | tf_op jit(solution)/shard_map/ppermute | solution.py:355
  79.6 7.3 %collective-permute-start.15 = (bf16[104,512]{1,0:T(8,128)(2,1)S(1)}, bf16[104,512]{1,0:T(8,128)(2,1)S(1)}, u32[]{:S(2)}, u32[]{:S(2)}) collective-permute-start(bf16[104,512]{1,0:T(8,128)(2,1)S(1)} %add_convert_fusion), channel_id=1, source_target_pairs={{0,2},{1,3},{2,0},{3,1},{4,6},{5,7},{6,4},{7,5},{8,10},{9,11},{10,... | collective-permute-start | bytes 319496 | tf_op jit(solution)/shard_map/ppermute | solution.py:355
  82.3 6.1 %collective-permute-start.16 = (bf16[104,512]{1,0:T(8,128)(2,1)S(1)}, bf16[104,512]{1,0:T(8,128)(2,1)S(1)}, u32[]{:S(2)}, u32[]{:S(2)}) collective-permute-start(bf16[104,512]{1,0:T(8,128)(2,1)S(1)} %add_convert_fusion), channel_id=1, source_target_pairs={{0,3},{1,2},{2,1},{3,0},{4,7},{5,6},{6,5},{7,4},{8,11},{9,10},{10,... | collective-permute-start | bytes 319496 | tf_op jit(solution)/shard_map/ppermute | solution.py:355
